TPU v7x, 512 devices: a whole 4x4x16 slice. The times are simulated.
512 devices in a mesh: role: 4 (over y), rows: 128 (over x, z, core).
Axes of the slice: x: 4, y: 4, z: 16, core: 2. Of those that a mesh axis runs over, the one named last changes fastest.
Arguments:
- embeddings: float32 [32768, 1024], P('rows'), may hold values from -6 to 6
- earlier_factor: float32 [32768, 256], P('rows', 'role'), may hold values from -0.5 to 0.5
- block_of: int32 [128], replicated, may hold values from 0 to 127, each once
Outputs:
- factor_panels: float32 [32768, 2, 256], P('rows', None, 'role')
Inputs may be any that keep to these rules, and one draw needn't show every extreme that they name: `block_of`: a permutation: each matrix row block 0 to 127 sits at exactly one stored block position.
All inputs are finite; a program needn't handle non-finite values.
Results may differ from a plain program's by a relative error of at most 0.0003.
Values sent between devices are 32-bit elements; how exact they have to be, the bound alone decides.
No kernel may reach another device: no remote copies, remote signals or barrier semaphores. Data moves between devices by JAX's collectives and lax.ppermute only.
A program may use at most 64 MiB of HBM per device.

v0:
```python
import jax
import jax.numpy as jnp
from jax import lax
from jax.experimental import pallas as pl
from jax.sharding import Mesh
from jax.sharding import PartitionSpec as P

ROWS = ("x", "far", "near", "core")

highest = lax.Precision.HIGHEST
ridge_weight = 1.0
TILE = 64
STEP = 8


def outer_rows(rows, columns):
    return lax.dot_general(
        rows,
        columns,
        (((1,), (1,)), ((), ())),
        precision=highest,
        preferred_element_type=jnp.float32,
    )


def product(left, right):
    return lax.dot_general(
        left,
        right,
        (((1,), (0,)), ((), ())),
        precision=highest,
        preferred_element_type=jnp.float32,
    )


def exchange(array, axis):
    return lax.all_to_all(array, axis, 0, 0, tiled=True)


def copies_from(array, axis):
    count = lax.axis_size(axis)
    return exchange(jnp.broadcast_to(array[None], (count, *array.shape)), axis)


def pick(array, index):
    return lax.dynamic_index_in_dim(array, index, 0, keepdims=False)


def small_inverse(block):
    size = block.shape[0]
    row_ids = lax.broadcasted_iota(jnp.int32, (size, size), 0)
    col_ids = lax.broadcasted_iota(jnp.int32, (size, size), 1)
    identity = (row_ids == col_ids).astype(jnp.float32)
    both = jnp.concatenate([block, identity], axis=1)
    tiles = [both[STEP * g : STEP * g + STEP] for g in range(size // STEP)]
    shape = tiles[0].shape
    lane = lax.broadcasted_iota(jnp.int32, shape, 0)
    pivots = [None] * len(tiles)
    for g in range(len(tiles)):
        later = range(g, len(tiles))
        start = STEP * g
        cols = [
            {h: jnp.broadcast_to(tiles[h][:, start + q : start + q + 1], shape) for h in later}
            for q in range(STEP)
        ]
        rows = [jnp.broadcast_to(tiles[g][a : a + 1], shape) for a in range(STEP)]
        piv = [
            [jnp.broadcast_to(cols[b][g][a : a + 1], shape) for b in range(a + 1)]
            for a in range(STEP)
        ]
        inverse = [None] * STEP
        for q in range(STEP):
            if q % 2 == 0:
                inverse[q] = 1.0 / piv[q][q]
                inverse[q + 1] = piv[q][q] / (
                    piv[q][q] * piv[q + 1][q + 1] - piv[q + 1][q] * piv[q + 1][q]
                )
            for a in range(q + 1, STEP):
                ratio = piv[a][q] * inverse[q]
                for b in range(q + 1, a + 1):
                    piv[a][b] = piv[a][b] - ratio * piv[b][q]
                rows[a] = rows[a] - ratio * rows[q]
                for h in later:
                    cols[a][h] = cols[a][h] - ratio * cols[q][h]
        pivots[g] = piv[0][0]
        for q in range(1, STEP):
            pivots[g] = jnp.where(lane == q, piv[q][q], pivots[g])
        for h in later:
            for q in range(STEP):
                if h == g and q == STEP - 1:
                    continue
                factor = cols[q][h] * inverse[q]
                if h == g:
                    factor = jnp.where(lane > q, factor, 0.0)
                tiles[h] = tiles[h] - factor * rows[q]
    done = [t[:, size:] * lax.rsqrt(p[:, size:]) for t, p in zip(tiles, pivots)]
    return jnp.concatenate(done, axis=0)


def factor_inverse(whole):
    count = whole.shape[0] // TILE
    left = [
        [whole[TILE * i : TILE * i + TILE, TILE * j : TILE * j + TILE] for j in range(count)]
        for i in range(count)
    ]
    lower = [[None] * count for _ in range(count)]
    inverse = [[jnp.zeros((TILE, TILE), jnp.float32)] * count for _ in range(count)]
    for k in range(count):
        inverse[k][k] = small_inverse(left[k][k])
        for i in range(k + 1, count):
            lower[i][k] = outer_rows(left[i][k], inverse[k][k])
        for i in range(k + 1, count):
            for j in range(k + 1, i + 1):
                left[i][j] = left[i][j] - outer_rows(lower[i][k], lower[j][k])
        for j in range(k):
            total = product(lower[k][j], inverse[j][j])
            for m in range(j + 1, k):
                total = total + product(lower[k][m], inverse[m][j])
            inverse[k][j] = -product(inverse[k][k], total)
    return jnp.concatenate([jnp.concatenate(row, axis=1) for row in inverse], axis=0)


def factor_kernel(top_ref, side_ref, low_ref, first_ref, below_ref, second_ref):
    first = factor_inverse(top_ref[...])
    first_ref[...] = first
    below = outer_rows(side_ref[...], first)
    below_ref[...] = below
    second_ref[...] = factor_inverse(low_ref[...] - outer_rows(below, below))


def factors(top, side, low):
    square = jax.ShapeDtypeStruct(top.shape, jnp.float32)
    return pl.pallas_call(
        factor_kernel, out_shape=(square, square, square), name="factors"
    )(top, side, low)


def broadcast_panels(payload, owners):
    far_count, near_count = lax.axis_size("far"), lax.axis_size("near")
    x_count, core_count = lax.axis_size("x"), lax.axis_size("core")
    role_count = lax.axis_size("role")
    rows, width = payload.shape
    groups = near_count * x_count
    high, half = rows // groups, width // core_count
    pieces = payload.reshape(groups, high, core_count, half)
    pieces = pieces.transpose(0, 2, 1, 3).reshape(groups * core_count, high, half)
    seen = exchange(pieces, ("near", "x", "core"))
    sources, fars = [], []
    for owner in owners:
        core, place = owner % core_count, owner // core_count
        near, place = place % near_count, place // near_count
        far, x = place % far_count, place // far_count
        sources.append((near * x_count + x) * core_count + core)
        fars.append(far)
    own = jnp.stack([pick(seen, source) for source in sources])
    seen = copies_from(own.reshape(-1, half), "far").reshape(far_count, *own.shape)
    own = jnp.stack([pick(seen[:, p], far) for p, far in enumerate(fars)])
    strip = copies_from(own.reshape(-1, half), "near")
    mine = copies_from(strip, ("role", "x"))
    other = lax.ppermute(mine, "core", [(0, 1), (1, 0)])
    first = lax.axis_index("core") == 0
    both = jnp.stack([jnp.where(first, mine, other), jnp.where(first, other, mine)])
    both = both.reshape(core_count, role_count, x_count, near_count, len(owners), high, half)
    both = both.transpose(4, 1, 3, 2, 5, 0, 6)
    return both.reshape(len(owners), role_count * rows, width)


def kernel_of(row_points, row_norms, col_points, col_norms, scale):
    inner = outer_rows(row_points, col_points)
    return jnp.exp(-(row_norms[:, None] + col_norms[None, :] - 2.0 * inner) / scale)


def ridge(size):
    return ridge_weight * jnp.eye(size, dtype=jnp.float32)


def on_device(embeddings, earlier_factor, block_of):
    size, width = embeddings.shape
    role_count = lax.axis_size("role")
    columns = size // role_count
    role = lax.axis_index("role")
    slot = lax.axis_index(ROWS)
    my_block = lax.dynamic_index_in_dim(block_of, slot, 0, keepdims=False)
    slots = jnp.arange(block_of.shape[0], dtype=jnp.int32)
    owners = [jnp.sum(jnp.where(block_of == panel, slots, 0)) for panel in range(2)]

    own_points = lax.dynamic_slice_in_dim(embeddings, role * columns, columns, 0)
    known_wide = jnp.concatenate(
        [earlier_factor[g * columns : (g + 1) * columns] for g in range(role_count)], axis=1
    )
    payload = jnp.concatenate([own_points, known_wide], axis=1)
    panels = broadcast_panels(payload, owners)
    known = copies_from(earlier_factor, "role")
    known = known.transpose(1, 0, 2).reshape(size, size)

    points, knowns = [], []
    for panel in panels:
        points.append(panel[:, :width])
        part = panel[:, width:].reshape(role_count, columns, role_count, columns)
        knowns.append(part.transpose(2, 1, 0, 3).reshape(size, size))

    scale = 2.0 * width
    norms = [jnp.sum(p * p, axis=1) for p in points]
    row_norms = jnp.sum(embeddings * embeddings, axis=1)

    def schur(rows, rows_norm, rows_known, panel):
        kernel = kernel_of(rows, rows_norm, points[panel], norms[panel], scale)
        return kernel - outer_rows(rows_known, knowns[panel])

    first_rows = schur(embeddings, row_norms, known, 0) + jnp.where(my_block == 0, ridge(size), 0.0)
    second_rows = schur(embeddings, row_norms, known, 1) + jnp.where(my_block == 1, ridge(size), 0.0)
    top = schur(points[0], norms[0], knowns[0], 0) + ridge(size)
    side = schur(points[1], norms[1], knowns[1], 0)
    low = schur(points[1], norms[1], knowns[1], 1) + ridge(size)

    top_inverse, below, low_inverse = factors(top, side, low)
    first_panel = outer_rows(first_rows, top_inverse)
    second_rows = second_rows - outer_rows(first_panel, below)
    own_inverse = lax.dynamic_slice_in_dim(low_inverse, role * columns, columns, 0)
    second_panel = outer_rows(second_rows, own_inverse)
    second_panel = jnp.where(my_block < 1, 0.0, second_panel)
    first_panel = lax.dynamic_slice_in_dim(first_panel, role * columns, columns, 1)
    return jnp.stack([first_panel, second_panel], axis=1)


def solution(mesh):
    finer = Mesh(
        mesh.devices.reshape(mesh.shape["role"], 4, 4, 4, 2), ("role", *ROWS)
    )
    placed = (P(ROWS, None), P(ROWS, "role"), P())
    return jax.shard_map(
        on_device, mesh=finer, in_specs=placed, out_specs=P(ROWS, None, "role"), check_vma=False
    )
```

profile of v0, /device:TPU:1, one launch (start us, length us, event | category | flops | bytes accessed | tf_op | source)
XLA Modules:
  0.0 160.2 jit_solution(4786501366358029452)
XLA Ops:
  3.3 10.4 %all-to-all-start = ((f32[32,4,640]{2,1,0:T(4,128)}), f32[32,4,640]{2,1,0:T(4,128)S(1)}, u32[]{:S(2)}, u32[]{:S(2)}) async-start(f32[32,4,640]{2,1,0:T(4,128)} %bitcast.1), calls=%async_computation | async-start | bytes 655360 | tf_op jit(solution)/shard_map/all_to_all | solution.py:37
  19.4 6.9 %all-to-all-done = f32[32,4,640]{2,1,0:T(4,128)S(1)} async-done(((f32[32,4,640]{2,1,0:T(4,128)}), f32[32,4,640]{2,1,0:T(4,128)S(1)}, u32[]{:S(2)}, u32[]{:S(2)}) %all-to-all-start) | async-done | bytes 327712 | tf_op jit(solution)/shard_map/all_to_all | solution.py:37
  26.9 11.6 %all-to-all-start.1 = ((f32[4,8,640]{2,1,0:T(8,128)}), f32[4,8,640]{2,1,0:T(8,128)S(1)}, u32[]{:S(2)}, u32[]{:S(2)}) async-start(f32[4,8,640]{2,1,0:T(8,128)} %broadcast_in_dim.24), calls=%async_computation.1 | async-start | bytes 163840 | tf_op jit(solution)/shard_map/all_to_all | solution.py:37
  38.6 11.8 %all-to-all-done.1 = f32[4,8,640]{2,1,0:T(8,128)S(1)} async-done(((f32[4,8,640]{2,1,0:T(8,128)}), f32[4,8,640]{2,1,0:T(8,128)S(1)}, u32[]{:S(2)}, u32[]{:S(2)}) %all-to-all-start.1) | async-done | bytes 81952 | tf_op jit(solution)/shard_map/all_to_all | solution.py:37
  50.5 7.0 %all_to_all.25 = f32[4,8,640]{2,1,0:T(8,128)S(1)} all-to-all(f32[4,8,640]{2,1,0:T(8,128)S(1)} %broadcast_in_dim.26), channel_id=1, replica_groups=mesh['role'=4,'x'=4,'far'=4,'near'=4,'core'=2] {'near'}, dimensions={0} | all-to-all | bytes 163840 | tf_op jit(solution)/shard_map/all_to_all | solution.py:37
  57.8 22.7 %all_to_all.26 = f32[16,4,8,640]{3,1,2,0:T(4,128)S(1)} all-to-all(f32[16,4,8,640]{3,1,2,0:T(4,128)S(1)} %broadcast_in_dim.27), channel_id=1, replica_groups=mesh['role'=4,'x'=4,'far'=4,'near'=4,'core'=2] {'role','x'}, dimensions={0} | all-to-all | bytes 2621440 | tf_op jit(solution)/shard_map/all_to_all | solution.py:37
  80.5 6.1 %collective-permute-start = (f32[16,4,8,640]{3,1,2,0:T(4,128)S(1)}, f32[16,4,8,640]{3,1,2,0:T(4,128)}, u32[]{:S(2)}, u32[]{:S(2)}) collective-permute-start(f32[16,4,8,640]{3,1,2,0:T(4,128)S(1)} %all_to_all.26), channel_id=1, source_target_pairs={{0,1},{1,0},{2,3},{3,2},{4,5},{5,4},{6,7},{7,6},{8,9},{9,8},{10,11... | collective-permute-start | bytes 3932168 | tf_op jit(solution)/shard_map/ppermute | solution.py:160
  87.3 4.2 %all-to-all-start.4 = ((f32[4,256,64]{1,2,0:T(8,128)}), f32[4,256,64]{1,2,0:T(8,128)}, u32[]{:S(2)}, u32[]{:S(2)}) async-start(f32[4,256,64]{1,2,0:T(8,128)} %broadcast_in_dim.28), calls=%async_computation.4 | async-start | bytes 524288 | tf_op jit(solution)/shard_map/all_to_all | solution.py:37
  94.4 1.5 broadcast_select_fusion.1
  101.5 1.8 %fusion.16 = f32[256,256]{0,1:T(8,128)} fusion(f32[256,1280]{1,0:T(8,128)S(1)} %bitcast.89, f32[256,1280]{1,0:T(8,128)S(1)} %bitcast.84, f32[256]{0:T(256)S(1)} %multiply_reduce_fusion, f32[256]{0:T(256)S(1)} %multiply_reduce_fusion.1), kind=kOutput, calls=%fused_computation.26 | convolution fusion | flops 805634048 | bytes 2361344 | tf_op jit(solution)/shard_map/dot_general | solution.py:17
  103.2 1.8 %fusion.20 = f32[256,256]{0,1:T(8,128)} fusion(f32[256,1280]{1,0:T(8,128)S(1)} %bitcast.85, f32[256]{0:T(256)S(1)} %multiply_reduce_fusion.1), kind=kOutput, calls=%fused_computation.31 | convolution fusion | flops 805634048 | bytes 1312768 | tf_op jit(solution)/shard_map/dot_general | solution.py:17
  105.1 1.7 %fusion.12 = f32[256,256]{1,0:T(8,128)} fusion(f32[256,256]{1,0:T(8,128)S(1)} %copy.95, f32[256,1280]{1,0:T(8,128)S(1)} %bitcast.90), kind=kOutput, calls=%fused_computation.21 | convolution fusion | flops 805568512 | bytes 1572864 | tf_op jit(solution)/shard_map/dot_general | solution.py:17
  110.6 2.0 %reshape.54 = f32[4,64,4,64]{3,2,1,0:T(4,128)} reshape(f32[256,256]{1,0:T(8,128)} %slice.45) | data formatting | bytes 524288 | tf_op jit(solution)/shard_map/reshape | solution.py:199
  112.6 2.2 %copy.114 = f32[4,64,4,64]{3,0,1,2:T(4,128)} copy(f32[4,64,4,64]{3,2,1,0:T(4,128)} %reshape.54) | data formatting | bytes 524288 | tf_op jit(solution)/shard_map/reshape | solution.py:199
  116.1 2.1 %fusion.2.low_ref = f32[256,256]{1,0:T(8,128)} fusion(f32[256,256]{1,0:T(8,128)} %fusion.12, f32[256,256]{1,0:T(8,128)S(1)} %reshape.58), kind=kOutput, calls=%fused_computation.6 | convolution fusion | flops 201588736 | bytes 786432 | tf_op jit(solution)/shard_map/dot_general | solution.py:17
  118.2 2.1 %convolution_subtract_fusion.2 = f32[256,256]{0,1:T(8,128)} fusion(f32[256,256]{0,1:T(8,128)} %fusion.16, f32[256,256]{1,0:T(8,128)S(1)} %reshape.58, f32[256,256]{1,0:T(8,128)S(1)} %reshape.55), kind=kOutput, calls=%fused_computation.7 | convolution fusion | flops 201392128 | bytes 1048576 | tf_op jit(solution)/shard_map/dot_general | solution.py:17
  120.2 1.8 %copy.97.side_ref = f32[256,256]{1,0:T(8,128)} copy(f32[256,256]{0,1:T(8,128)} %convolution_subtract_fusion.2) | data formatting | bytes 524288 | tf_op jit(solution)/shard_map/sub | solution.py:208
  122.0 2.1 %fusion.3 = f32[256,256]{0,1:T(8,128)} fusion(f32[256,256]{0,1:T(8,128)S(1)} %copy.83, f32[256,256]{0,1:T(8,128)} %fusion.20, f32[256,256]{1,0:T(8,128)S(1)} %reshape.55), kind=kOutput, calls=%fused_computation.9 | convolution fusion | flops 201457664 | bytes 1048576 | tf_op jit(solution)/shard_map/dot_general | solution.py:17
  124.1 1.8 %copy.96.top_ref = f32[256,256]{1,0:T(8,128)} copy(f32[256,256]{0,1:T(8,128)} %fusion.3) | data formatting | bytes 524288 | tf_op jit(solution)/shard_map/add | solution.py:212
  125.9 3.0 %fusion.8 = f32[256,256]{0,1:T(8,128)} fusion(f32[256,1024]{1,0:T(8,128)} %param.3, f32[256,1280]{1,0:T(8,128)S(1)} %bitcast.91, f32[256]{0:T(256)S(1)} %multiply_reduce_fusion, f32[256]{0:T(256)S(1)} %multiply_reduce_fusion.2), kind=kOutput, calls=%fused_computation.16 | convolution fusion | flops 805568512 | bytes 2361344 | tf_op jit(solution)/shard_map/dot_general | solution.py:17
  130.0 22.4 %factors.1 = (f32[256,256]{1,0:T(8,128)}, f32[256,256]{1,0:T(8,128)}, f32[256,256]{1,0:T(8,128)}) custom-call(f32[256,256]{1,0:T(8,128)} %copy.96.top_ref, f32[256,256]{1,0:T(8,128)} %copy.97.side_ref, f32[256,256]{1,0:T(8,128)} %fusion.2.low_ref), custom_call_target="tpu_custom_call" | custom-call | tf_op jit(solution)/shard_map/factors/pallas_call | solution.py:133
  152.5 1.8 %fusion.25 = f32[256,256]{0,1:T(8,128)} fusion(f32[256,1024]{1,0:T(8,128)S(1)} %copy-done.1, f32[256,1280]{1,0:T(8,128)S(1)} %bitcast.86, f32[256]{0:T(256)S(1)} %multiply_reduce_fusion.1, f32[256]{0:T(256)S(1)} %multiply_reduce_fusion.2), kind=kOutput, calls=%fused_computation.37 | convolution fusion | flops 805634048 | bytes 2361344 | tf_op jit(solution)/shard_map/dot_general | solution.py:17
  154.2 1.5 fusion.5
  156.1 1.5 fusion.1
  (63 shorter events, 21.3 us)
Async XLA Ops:
  2.2 11.5 %copy-start.5 = (s32[128]{0:T(128)S(1)}, s32[128]{0:T(128)}, u32[]{:S(2)}) copy-start(s32[128]{0:T(128)} %param.5) | copy-start | bytes 1540
  3.3 22.9 %all-to-all-start = ((f32[32,4,640]{2,1,0:T(4,128)}), f32[32,4,640]{2,1,0:T(4,128)S(1)}, u32[]{:S(2)}, u32[]{:S(2)}) async-start(f32[32,4,640]{2,1,0:T(4,128)} %bitcast.1), calls=%async_computation | async-start | bytes 655360 | tf_op jit(solution)/shard_map/all_to_all | solution.py:37
  26.9 23.4 %all-to-all-start.1 = ((f32[4,8,640]{2,1,0:T(8,128)}), f32[4,8,640]{2,1,0:T(8,128)S(1)}, u32[]{:S(2)}, u32[]{:S(2)}) async-start(f32[4,8,640]{2,1,0:T(8,128)} %broadcast_in_dim.24), calls=%async_computation.1 | async-start | bytes 163840 | tf_op jit(solution)/shard_map/all_to_all | solution.py:37
  57.8 28.9 %copy-start.2 = (f32[256,64]{0,1:T(8,128)S(1)}, f32[256,64]{0,1:T(8,128)}, u32[]{:S(2)}) copy-start(f32[256,64]{0,1:T(8,128)} %param.4) | copy-start | bytes 196612
  80.5 13.8 %copy-start = (f32[256,1024]{1,0:T(8,128)S(1)}, f32[256,1024]{1,0:T(8,128)}, u32[]{:S(2)}) copy-start(f32[256,1024]{1,0:T(8,128)} %param.3) | copy-start | bytes 3145732
  80.5 14.0 %collective-permute-start = (f32[16,4,8,640]{3,1,2,0:T(4,128)S(1)}, f32[16,4,8,640]{3,1,2,0:T(4,128)}, u32[]{:S(2)}, u32[]{:S(2)}) collective-permute-start(f32[16,4,8,640]{3,1,2,0:T(4,128)S(1)} %all_to_all.26), channel_id=1, source_target_pairs={{0,1},{1,0},{2,3},{3,2},{4,5},{5,4},{6,7},{7,6},{8,9},{9,8},{10,11... | collective-permute-start | bytes 3932168 | tf_op jit(solution)/shard_map/ppermute | solution.py:160
  87.3 66.9 %all-to-all-start.4 = ((f32[4,256,64]{1,2,0:T(8,128)}), f32[4,256,64]{1,2,0:T(8,128)}, u32[]{:S(2)}, u32[]{:S(2)}) async-start(f32[4,256,64]{1,2,0:T(8,128)} %broadcast_in_dim.28), calls=%async_computation.4 | async-start | bytes 524288 | tf_op jit(solution)/shard_map/all_to_all | solution.py:37
  128.8 23.6 %copy-start.1 = (f32[256,1024]{1,0:T(8,128)S(1)}, f32[256,1024]{1,0:T(8,128)}, u32[]{:S(2)}) copy-start(f32[256,1024]{1,0:T(8,128)} %param.3) | copy-start | bytes 3145732
  154.2 1.5 copy-start.3
  155.7 2.0 %copy-start.4 = (f32[256,256]{1,0:T(8,128)S(1)}, f32[256,256]{1,0:T(8,128)}, u32[]{:S(2)}) copy-start(f32[256,256]{1,0:T(8,128)} %get-tuple-element.9) | copy-start | bytes 786436
where the time goes:
time: 161 us; the launch traced here: 160 us
  starting transfers between devices  32.3 us (20%)
  blocking collectives  29.7 us (18%)
  local copies, waits for them, and re-layouts  24.2 us (15%)
  Pallas kernels  22.4 us (14%)
  matrix products  21.4 us (13%)
  waiting for transfers between devices  18.7 us (12%)
  between operations  7.31 us (5%)
  other arithmetic  4.17 us (3%)
    all_to_all x2, blocking collectives, exchange(): return lax.all_to_all(array, axis, 0, 0, tiled=True)  29.7 us
    all_to_all x3, starting transfers between devices, exchange(): return lax.all_to_all(array, axis, 0, 0, tiled=True)  26.2 us
    pallas_call x1, Pallas kernels, factors(): pl.pallas_call(factor_kernel, out_shape=(square, square, square), name='f...  22.4 us
    dot_general x13, matrix products, outer_rows(): lax.dot_general(rows, columns, (((1,), (1,)), ((), ())), precision=highes...  21.4 us
    all_to_all x3, waiting for transfers between devices, exchange(): return lax.all_to_all(array, axis, 0, 0, tiled=True)  18.7 us
    reshape x4, local copies, waits for them, and re-layouts, on_device(): part = panel[:, width:].reshape(role_count, columns, role_count, columns)  6.46 us
    ppermute x1, starting transfers between devices, broadcast_panels(): other = lax.ppermute(mine, 'core', [(0, 1), (1, 0)])  6.11 us
  transfers between devices with their start and end apart: 4, of which 2 were waited for; matrix products, arithmetic and copies ran while one was open for 25% of the time, Pallas kernels for 14%

commit v1 on v0

--- a/solution.py
+++ b/solution.py
@@ -2,6 +2,7 @@
 import jax.numpy as jnp
 from jax import lax
 from jax.experimental import pallas as pl
+from jax.experimental.pallas import tpu as pltpu
 from jax.sharding import Mesh
 from jax.sharding import PartitionSpec as P
 
@@ -120,31 +121,129 @@
     return jnp.concatenate([jnp.concatenate(row, axis=1) for row in inverse], axis=0)
 
 
-def factor_kernel(top_ref, side_ref, low_ref, first_ref, below_ref, second_ref):
-    first = factor_inverse(top_ref[...])
-    first_ref[...] = first
-    below = outer_rows(side_ref[...], first)
-    below_ref[...] = below
-    second_ref[...] = factor_inverse(low_ref[...] - outer_rows(below, below))
-
-
-def factors(top, side, low):
-    square = jax.ShapeDtypeStruct(top.shape, jnp.float32)
+def gathered_rows(parts):
+    count = parts.shape[1] // TILE
+    rows = []
+    for g in range(count):
+        rows.append(
+            jnp.concatenate(
+                [
+                    parts[TILE * c : TILE * c + TILE, TILE * g : TILE * g + TILE]
+                    for c in range(count)
+                ],
+                axis=1,
+            )
+        )
+    return jnp.concatenate(rows, axis=0)
+
+
+def finish_kernel(
+    flags_ref,
+    mine_ref,
+    other_ref,
+    embeddings_ref,
+    parts_ref,
+    first_ref,
+    second_ref,
+    points_ref,
+    raw_ref,
+    inverse_ref,
+):
+    size, width = embeddings_ref.shape
+    half = mine_ref.shape[-1]
+    split = width - half
+    is_first = flags_ref[0] == 0
+
+    def place(step, _):
+        c, near = step // 4, step % 4
+        for pair in range(2):
+            row = pl.multiple_of(step * 16 + pair * 8, 8)
+            for k in range(2):
+                mine = [mine_ref[4 * c + 2 * pair + e, near] for e in range(2)]
+                other = [other_ref[4 * c + 2 * pair + e, near] for e in range(2)]
+                use_mine = is_first if k == 0 else jnp.logical_not(is_first)
+                even, odd = [jnp.where(use_mine, m, o) for m, o in zip(mine, other)]
+                for p in range(2):
+                    rows = jnp.concatenate(
+                        [even[4 * p : 4 * p + 4], odd[4 * p : 4 * p + 4]], axis=0
+                    )
+                    if k == 0:
+                        points_ref[p, pl.ds(row, 8), :half] = rows
+                    else:
+                        points_ref[p, pl.ds(row, 8), half:] = rows[:, :split]
+                        raw_ref[p, pl.ds(row, 8), :] = rows[:, split:]
+        return 0
+
+    lax.fori_loop(0, 16, place, 0)
+    scale = -1.0 / (2.0 * width)
+    row_ids = lax.broadcasted_iota(jnp.int32, (size, size), 0)
+    col_ids = lax.broadcasted_iota(jnp.int32, (size, size), 1)
+    ridge = jnp.where(row_ids == col_ids, ridge_weight, 0.0)
+    points = [points_ref[p] for p in range(2)]
+    knowns = [gathered_rows(raw_ref[p]) for p in range(2)]
+    known = gathered_rows(parts_ref[...])
+    embeddings = embeddings_ref[...]
+    ones = jnp.ones((8, width), jnp.float32)
+    col_norms = [outer_rows(ones, p * p)[:1] for p in points]
+    norms = [jnp.sum(p * p, axis=1, keepdims=True) for p in points]
+    row_norms = jnp.sum(embeddings * embeddings, axis=1, keepdims=True)
+
+    def schur(rows, rows_norm, rows_known, panel):
+        inner = outer_rows(rows, points[panel])
+        kernel = jnp.exp((rows_norm + col_norms[panel] - 2.0 * inner) * scale)
+        return kernel - outer_rows(rows_known, knowns[panel])
+
+    top = schur(points[0], norms[0], knowns[0], 0) + ridge
+    first = factor_inverse(top)
+    inverse_ref[0] = first
+    side = schur(points[1], norms[1], knowns[1], 0)
+    low = schur(points[1], norms[1], knowns[1], 1) + ridge
+    below = outer_rows(side, first)
+    inverse_ref[1] = factor_inverse(low - outer_rows(below, below))
+    first_rows = schur(embeddings, row_norms, known, 0)
+    first_rows = first_rows + jnp.where(flags_ref[1] == 0, ridge, 0.0)
+    second_rows = schur(embeddings, row_norms, known, 1)
+    second_rows = second_rows + jnp.where(flags_ref[1] == 1, ridge, 0.0)
+    first_panel = outer_rows(first_rows, first)
+    second_rows = second_rows - outer_rows(first_panel, below)
+    columns = first_ref.shape[1]
+    own = pl.ds(pl.multiple_of(flags_ref[2] * columns, 8), columns)
+    first_ref[...] = outer_rows(first_rows, inverse_ref[0, own, :])
+    second = outer_rows(second_rows, inverse_ref[1, own, :])
+    second_ref[...] = jnp.where(flags_ref[1] < 1, 0.0, second)
+
+
+def finish(flags, mine, other, embeddings, parts):
+    size, width = embeddings.shape
+    known = parts.shape[1]
+    columns = size // lax.axis_size("role")
+    out = jax.ShapeDtypeStruct((size, columns), jnp.float32)
+    whole = pl.BlockSpec(memory_space=pltpu.VMEM)
     return pl.pallas_call(
-        factor_kernel, out_shape=(square, square, square), name="factors"
-    )(top, side, low)
-
-
-def broadcast_panels(payload, owners):
+        finish_kernel,
+        in_specs=[pl.BlockSpec(memory_space=pltpu.SMEM)] + [whole] * 4,
+        out_specs=(whole, whole),
+        out_shape=(out, out),
+        scratch_shapes=[
+            pltpu.VMEM((2, size, width), jnp.float32),
+            pltpu.VMEM((2, size, known), jnp.float32),
+            pltpu.VMEM((2, size, size), jnp.float32),
+        ],
+        name="finish",
+    )(flags, mine, other, embeddings, parts)
+
+
+def broadcast_panels(payload, known_wide, owners):
     far_count, near_count = lax.axis_size("far"), lax.axis_size("near")
     x_count, core_count = lax.axis_size("x"), lax.axis_size("core")
-    role_count = lax.axis_size("role")
     rows, width = payload.shape
     groups = near_count * x_count
     high, half = rows // groups, width // core_count
     pieces = payload.reshape(groups, high, core_count, half)
     pieces = pieces.transpose(0, 2, 1, 3).reshape(groups * core_count, high, half)
     seen = exchange(pieces, ("near", "x", "core"))
+    parts = copies_from(known_wide, "role")
+    seen, parts = lax.optimization_barrier((seen, parts))
     sources, fars = [], []
     for owner in owners:
         core, place = owner % core_count, owner // core_count
@@ -152,30 +251,19 @@
         far, x = place % far_count, place // far_count
         sources.append((near * x_count + x) * core_count + core)
         fars.append(far)
-    own = jnp.stack([pick(seen, source) for source in sources])
-    seen = copies_from(own.reshape(-1, half), "far").reshape(far_count, *own.shape)
-    own = jnp.stack([pick(seen[:, p], far) for p, far in enumerate(fars)])
-    strip = copies_from(own.reshape(-1, half), "near")
+    own = jnp.concatenate([pick(seen, source) for source in sources], axis=0)
+    seen = copies_from(own, ("far", "near"))
+    seen = seen.reshape(far_count, near_count, len(owners) * high, half)
+    strips = [pick(seen, far) for far in fars]
+    sub = lax.broadcasted_iota(jnp.int32, strips[0].shape, 1)
+    strip = jnp.where(sub < high, strips[0], strips[1])
     mine = copies_from(strip, ("role", "x"))
     other = lax.ppermute(mine, "core", [(0, 1), (1, 0)])
-    first = lax.axis_index("core") == 0
-    both = jnp.stack([jnp.where(first, mine, other), jnp.where(first, other, mine)])
-    both = both.reshape(core_count, role_count, x_count, near_count, len(owners), high, half)
-    both = both.transpose(4, 1, 3, 2, 5, 0, 6)
-    return both.reshape(len(owners), role_count * rows, width)
-
-
-def kernel_of(row_points, row_norms, col_points, col_norms, scale):
-    inner = outer_rows(row_points, col_points)
-    return jnp.exp(-(row_norms[:, None] + col_norms[None, :] - 2.0 * inner) / scale)
-
-
-def ridge(size):
-    return ridge_weight * jnp.eye(size, dtype=jnp.float32)
+    return mine, other, parts
 
 
 def on_device(embeddings, earlier_factor, block_of):
-    size, width = embeddings.shape
+    size = embeddings.shape[0]
     role_count = lax.axis_size("role")
     columns = size // role_count
     role = lax.axis_index("role")
@@ -189,37 +277,10 @@
         [earlier_factor[g * columns : (g + 1) * columns] for g in range(role_count)], axis=1
     )
     payload = jnp.concatenate([own_points, known_wide], axis=1)
-    panels = broadcast_panels(payload, owners)
-    known = copies_from(earlier_factor, "role")
-    known = known.transpose(1, 0, 2).reshape(size, size)
-
-    points, knowns = [], []
-    for panel in panels:
-        points.append(panel[:, :width])
-        part = panel[:, width:].reshape(role_count, columns, role_count, columns)
-        knowns.append(part.transpose(2, 1, 0, 3).reshape(size, size))
-
-    scale = 2.0 * width
-    norms = [jnp.sum(p * p, axis=1) for p in points]
-    row_norms = jnp.sum(embeddings * embeddings, axis=1)
-
-    def schur(rows, rows_norm, rows_known, panel):
-        kernel = kernel_of(rows, rows_norm, points[panel], norms[panel], scale)
-        return kernel - outer_rows(rows_known, knowns[panel])
-
-    first_rows = schur(embeddings, row_norms, known, 0) + jnp.where(my_block == 0, ridge(size), 0.0)
-    second_rows = schur(embeddings, row_norms, known, 1) + jnp.where(my_block == 1, ridge(size), 0.0)
-    top = schur(points[0], norms[0], knowns[0], 0) + ridge(size)
-    side = schur(points[1], norms[1], knowns[1], 0)
-    low = schur(points[1], norms[1], knowns[1], 1) + ridge(size)
-
-    top_inverse, below, low_inverse = factors(top, side, low)
-    first_panel = outer_rows(first_rows, top_inverse)
-    second_rows = second_rows - outer_rows(first_panel, below)
-    own_inverse = lax.dynamic_slice_in_dim(low_inverse, role * columns, columns, 0)
-    second_panel = outer_rows(second_rows, own_inverse)
-    second_panel = jnp.where(my_block < 1, 0.0, second_panel)
-    first_panel = lax.dynamic_slice_in_dim(first_panel, role * columns, columns, 1)
+    mine, other, parts = broadcast_panels(payload, known_wide, owners)
+    flags = jnp.stack([lax.axis_index("core"), my_block, role])
+    parts = parts.reshape(size, -1)
+    first_panel, second_panel = finish(flags, mine, other, embeddings, parts)
     return jnp.stack([first_panel, second_panel], axis=1)
 
 

time: 161 us -> 132 us (0.82)
  matrix products: 21.4 us -> 0 us
  local copies, waits for them, and re-layouts: 24.2 us -> 7.45 us
  Pallas kernels: 22.4 us -> 32.5 us
  waiting for transfers between devices: 18.7 us -> 25.8 us
  blocking collectives: 29.7 us -> 22.7 us
  between operations: 7.31 us -> 5.28 us
  starting transfers between devices: 32.3 us -> 34.2 us
    dot_general x13 -> x0, matrix products: 21.4 us -> none  [outer_rows(): lax.dot_general(rows, columns, (((1,), (1,)), ((), ())), precision=highes...]
    pallas_call x1, Pallas kernels: 22.4 us -> 32.5 us  [finish(): pl.pallas_call(finish_kernel, in_specs=[pl.BlockSpec(memory_space=pltpu.S...]
    reshape x7 -> x0, local copies, waits for them, and re-layouts: 9.23 us -> none  [the longest x4 6.46 us: on_device(): part = panel[:, width:].reshape(role_count, columns, role_count, columns)]
    all_to_all x2 -> x1, blocking collectives: 29.7 us -> 22.7 us  [exchange(): return lax.all_to_all(array, axis, 0, 0, tiled=True)]
    all_to_all x3, waiting for transfers between devices: 18.7 us -> 25.2 us  [exchange(): return lax.all_to_all(array, axis, 0, 0, tiled=True)]
    another operation x3 -> x0, local copies, waits for them, and re-layouts: 2.7 us -> none
    add x2 -> x0, local copies, waits for them, and re-layouts: 1.91 us -> none  [the longest x1 1.79 us: on_device(): top = schur(points[0], norms[0], knowns[0], 0) + ridge(size)]
    sub x1 -> x0, local copies, waits for them, and re-layouts: 1.78 us -> none  [schur(): return kernel - outer_rows(rows_known, knowns[panel])]
  transfers between devices with their start and end apart: 4 -> 4, of which waited for: 2 -> 4; matrix products, arithmetic and copies ran while one was open for 25% -> 4% of each run, Pallas kernels for 14% -> 0%
where the time goes in v1:
time: 132 us; the launch traced here: 131 us
  starting transfers between devices  34.2 us (26%)
  Pallas kernels  32.5 us (25%)
  waiting for transfers between devices  25.8 us (20%)
  blocking collectives  22.7 us (17%)
  local copies, waits for them, and re-layouts  7.45 us (6%)
  between operations  5.28 us (4%)
  other arithmetic  3.12 us (2%)
    pallas_call x1, Pallas kernels, finish(): pl.pallas_call(finish_kernel, in_specs=[pl.BlockSpec(memory_space=pltpu.S...  32.5 us
    all_to_all x3, starting transfers between devices, exchange(): return lax.all_to_all(array, axis, 0, 0, tiled=True)  27.8 us
    all_to_all x3, waiting for transfers between devices, exchange(): return lax.all_to_all(array, axis, 0, 0, tiled=True)  25.2 us
    all_to_all x1, blocking collectives, exchange(): return lax.all_to_all(array, axis, 0, 0, tiled=True)  22.7 us
    ppermute x1, starting transfers between devices, broadcast_panels(): other = lax.ppermute(mine, 'core', [(0, 1), (1, 0)])  6.36 us
  transfers between devices with their start and end apart: 4, of which 4 were waited for; matrix products, arithmetic and copies ran while one was open for 4% of the time, Pallas kernels for 0%

profile of v1, /device:TPU:1, one launch (start us, length us, event | category | flops | bytes accessed | tf_op | source)
XLA Modules:
  0.0 131.2 jit_solution(17199544078554210429)
XLA Ops:
  0.0 0.9 fusion.2
  1.0 0.7 broadcast_in_dim.11
  1.7 5.0 %all-to-all-start.1 = ((f32[4,64,256]{2,1,0:T(8,128)}), f32[4,64,256]{2,1,0:T(8,128)S(1)}, u32[]{:S(2)}, u32[]{:S(2)}) async-start(f32[4,64,256]{2,1,0:T(8,128)} %broadcast_in_dim.11), calls=%async_computation.1 | async-start | bytes 524288 | tf_op jit(solution)/shard_map/all_to_all | solution.py:38
  7.1 1.0 constant_dynamic-slice_fusion
  8.1 0.1 concatenate.10
  8.2 0.2 reshape.14
  8.3 0.8 copy.14
  9.1 3.1 %all-to-all-done.1 = f32[4,64,256]{2,1,0:T(8,128)S(1)} async-done(((f32[4,64,256]{2,1,0:T(8,128)}), f32[4,64,256]{2,1,0:T(8,128)S(1)}, u32[]{:S(2)}, u32[]{:S(2)}) %all-to-all-start.1) | async-done | bytes 262176 | tf_op jit(solution)/shard_map/all_to_all | solution.py:38
  12.3 10.6 %all-to-all-start = ((f32[32,4,640]{2,1,0:T(4,128)}), f32[32,4,640]{2,1,0:T(4,128)S(1)}, u32[]{:S(2)}, u32[]{:S(2)}) async-start(f32[32,4,640]{2,1,0:T(4,128)} %bitcast.3), calls=%async_computation | async-start | bytes 655360 | tf_op jit(solution)/shard_map/all_to_all | solution.py:38
  22.9 0.7 fusion
  28.7 6.6 %all-to-all-done = f32[32,4,640]{2,1,0:T(4,128)S(1)} async-done(((f32[32,4,640]{2,1,0:T(4,128)}), f32[32,4,640]{2,1,0:T(4,128)S(1)}, u32[]{:S(2)}, u32[]{:S(2)}) %all-to-all-start) | async-done | bytes 327712 | tf_op jit(solution)/shard_map/all_to_all | solution.py:38
  35.3 0.7 broadcast_in_dim.12
  36.1 12.2 %all-to-all-start.2 = ((f32[16,8,640]{2,1,0:T(8,128)}), f32[16,8,640]{2,1,0:T(8,128)S(1)}, u32[]{:S(2)}, u32[]{:S(2)}) async-start(f32[16,8,640]{2,1,0:T(8,128)} %broadcast_in_dim.12), calls=%async_computation.2 | async-start | bytes 655360 | tf_op jit(solution)/shard_map/all_to_all | solution.py:38
  48.4 15.5 %all-to-all-done.2 = f32[16,8,640]{2,1,0:T(8,128)S(1)} async-done(((f32[16,8,640]{2,1,0:T(8,128)}), f32[16,8,640]{2,1,0:T(8,128)S(1)}, u32[]{:S(2)}, u32[]{:S(2)}) %all-to-all-start.2) | async-done | bytes 327712 | tf_op jit(solution)/shard_map/all_to_all | solution.py:38
  63.9 0.1 broadcast_in_dim.26
  64.1 22.7 %all_to_all.20.mine_ref = f32[16,4,8,640]{3,2,1,0:T(8,128)S(1)} all-to-all(f32[16,4,8,640]{3,2,1,0:T(8,128)S(1)} %broadcast_in_dim.26), channel_id=1, replica_groups=mesh['role'=4,'x'=4,'far'=4,'near'=4,'core'=2] {'role','x'}, dimensions={0} | all-to-all | bytes 2621440 | tf_op jit(solution)/shard_map/all_to_all | solution.py:38
  86.8 6.4 %collective-permute-start = (f32[16,4,8,640]{3,2,1,0:T(8,128)S(1)}, f32[16,4,8,640]{3,2,1,0:T(8,128)S(1)}, u32[]{:S(2)}, u32[]{:S(2)}) collective-permute-start(f32[16,4,8,640]{3,2,1,0:T(8,128)S(1)} %all_to_all.20.mine_ref), channel_id=1, source_target_pairs={{0,1},{1,0},{2,3},{3,2},{4,5},{5,4},{6,7},{7,6},{8,9},{9,8},{10,11... | collective-permute-start | bytes 3932168 | tf_op jit(solution)/shard_map/ppermute | solution.py:261
  93.2 0.7 dynamic_slice.21
  93.9 1.4 %pad_add_fusion.flags_ref = s32[3]{0:T(128)} fusion(s32[1]{0:T(128)} %bitcast.1, s32[1]{0:T(128)} %dynamic_slice.21, s32[1]{0:T(128)} %bitcast), kind=kLoop, calls=%fused_computation.11 | loop fusion | flops 6 | bytes 24 | tf_op jit(solution)/shard_map/stack | solution.py:281
  95.2 0.6 collective-permute-done.other_ref
  95.8 1.1 copy-done.1
  96.9 32.5 %finish.1 = (f32[256,64]{1,0:T(8,128)}, f32[256,64]{1,0:T(8,128)}) custom-call(s32[3]{0:T(128)} %pad_add_fusion.flags_ref, f32[16,4,8,640]{3,2,1,0:T(8,128)} %copy-done, f32[16,4,8,640]{3,2,1,0:T(8,128)} %copy-done.1, f32[256,1024]{1,0:T(8,128)} %embeddings_ref.1, f32[256,256]{1,0:T(8,128)} %bitcast.15), custom_call_target="tpu_custom_call" | custom-call | tf_op jit(solution)/shard_map/finish/pallas_call | solution.py:222
  129.4 1.0 pad_maximum_fusion
  130.4 0.8 copy.16
  (17 shorter events, 0.5 us)
Async XLA Ops:
  1.7 10.5 %all-to-all-start.1 = ((f32[4,64,256]{2,1,0:T(8,128)}), f32[4,64,256]{2,1,0:T(8,128)S(1)}, u32[]{:S(2)}, u32[]{:S(2)}) async-start(f32[4,64,256]{2,1,0:T(8,128)} %broadcast_in_dim.11), calls=%async_computation.1 | async-start | bytes 524288 | tf_op jit(solution)/shard_map/all_to_all | solution.py:38
  8.1 14.9 %copy-start.3 = (s32[128]{0:T(128)S(1)}, s32[128]{0:T(128)}, u32[]{:S(2)}) copy-start(s32[128]{0:T(128)} %param.5) | copy-start | bytes 1540
  12.3 51.8 %copy-start.2 = (f32[4,64,256]{2,1,0:T(8,128)}, f32[4,64,256]{2,1,0:T(8,128)S(1)}, u32[]{:S(2)}) copy-start(f32[4,64,256]{2,1,0:T(8,128)S(1)} %all-to-all-done.1) | copy-start | bytes 786436
  12.3 23.0 %all-to-all-start = ((f32[32,4,640]{2,1,0:T(4,128)}), f32[32,4,640]{2,1,0:T(4,128)S(1)}, u32[]{:S(2)}, u32[]{:S(2)}) async-start(f32[32,4,640]{2,1,0:T(4,128)} %bitcast.3), calls=%async_computation | async-start | bytes 655360 | tf_op jit(solution)/shard_map/all_to_all | solution.py:38
  36.1 27.8 %all-to-all-start.2 = ((f32[16,8,640]{2,1,0:T(8,128)}), f32[16,8,640]{2,1,0:T(8,128)S(1)}, u32[]{:S(2)}, u32[]{:S(2)}) async-start(f32[16,8,640]{2,1,0:T(8,128)} %broadcast_in_dim.12), calls=%async_computation.2 | async-start | bytes 655360 | tf_op jit(solution)/shard_map/all_to_all | solution.py:38
  86.8 9.0 %copy-start = (f32[16,4,8,640]{3,2,1,0:T(8,128)}, f32[16,4,8,640]{3,2,1,0:T(8,128)S(1)}, u32[]{:S(2)}) copy-start(f32[16,4,8,640]{3,2,1,0:T(8,128)S(1)} %all_to_all.20.mine_ref) | copy-start | bytes 3932164
  86.8 9.0 %collective-permute-start = (f32[16,4,8,640]{3,2,1,0:T(8,128)S(1)}, f32[16,4,8,640]{3,2,1,0:T(8,128)S(1)}, u32[]{:S(2)}, u32[]{:S(2)}) collective-permute-start(f32[16,4,8,640]{3,2,1,0:T(8,128)S(1)} %all_to_all.20.mine_ref), channel_id=1, source_target_pairs={{0,1},{1,0},{2,3},{3,2},{4,5},{5,4},{6,7},{7,6},{8,9},{9,8},{10,11... | collective-permute-start | bytes 3932168 | tf_op jit(solution)/shard_map/ppermute | solution.py:261
  95.8 1.1 copy-start.1

commit v2 on v1

--- a/solution.py
+++ b/solution.py
@@ -87,13 +87,15 @@
         for q in range(1, STEP):
             pivots[g] = jnp.where(lane == q, piv[q][q], pivots[g])
         for h in later:
-            for q in range(STEP):
-                if h == g and q == STEP - 1:
-                    continue
+            terms = []
+            for q in range(STEP - 1 if h == g else STEP):
                 factor = cols[q][h] * inverse[q]
                 if h == g:
                     factor = jnp.where(lane > q, factor, 0.0)
-                tiles[h] = tiles[h] - factor * rows[q]
+                terms.append(factor * rows[q])
+            while len(terms) > 1:
+                terms = [sum(terms[i : i + 2]) for i in range(0, len(terms), 2)]
+            tiles[h] = tiles[h] - terms[0]
     done = [t[:, size:] * lax.rsqrt(p[:, size:]) for t, p in zip(tiles, pivots)]
     return jnp.concatenate(done, axis=0)
 
@@ -121,38 +123,34 @@
     return jnp.concatenate([jnp.concatenate(row, axis=1) for row in inverse], axis=0)
 
 
-def gathered_rows(parts):
-    count = parts.shape[1] // TILE
-    rows = []
-    for g in range(count):
-        rows.append(
-            jnp.concatenate(
-                [
-                    parts[TILE * c : TILE * c + TILE, TILE * g : TILE * g + TILE]
-                    for c in range(count)
-                ],
-                axis=1,
-            )
-        )
-    return jnp.concatenate(rows, axis=0)
+def mesh_slot():
+    slot = 0
+    for axis in ROWS:
+        slot = slot * lax.axis_size(axis) + lax.axis_index(axis)
+    return slot
 
 
 def finish_kernel(
-    flags_ref,
+    block_ref,
     mine_ref,
     other_ref,
     embeddings_ref,
-    parts_ref,
-    first_ref,
-    second_ref,
+    part_ref,
+    near_ref,
+    across_ref,
+    back_ref,
+    out_ref,
     points_ref,
-    raw_ref,
+    known_ref,
     inverse_ref,
 ):
     size, width = embeddings_ref.shape
     half = mine_ref.shape[-1]
     split = width - half
-    is_first = flags_ref[0] == 0
+    columns = part_ref.shape[0]
+    is_first = lax.axis_index("core") == 0
+    role = lax.axis_index("role")
+    my_block = block_ref[mesh_slot()]
 
     def place(step, _):
         c, near = step // 4, step % 4
@@ -171,17 +169,19 @@
                         points_ref[p, pl.ds(row, 8), :half] = rows
                     else:
                         points_ref[p, pl.ds(row, 8), half:] = rows[:, :split]
-                        raw_ref[p, pl.ds(row, 8), :] = rows[:, split:]
+                        known_ref[p, pl.ds(row, 8), :] = rows[:, split:]
         return 0
 
     lax.fori_loop(0, 16, place, 0)
+    for step, ref in enumerate((part_ref, near_ref, across_ref, back_ref)):
+        source = lax.rem(role + 4 - step, 4)
+        known_ref[2, pl.ds(pl.multiple_of(source * columns, 8), columns), :] = ref[...]
     scale = -1.0 / (2.0 * width)
     row_ids = lax.broadcasted_iota(jnp.int32, (size, size), 0)
     col_ids = lax.broadcasted_iota(jnp.int32, (size, size), 1)
     ridge = jnp.where(row_ids == col_ids, ridge_weight, 0.0)
     points = [points_ref[p] for p in range(2)]
-    knowns = [gathered_rows(raw_ref[p]) for p in range(2)]
-    known = gathered_rows(parts_ref[...])
+    knowns = [known_ref[p] for p in range(2)]
     embeddings = embeddings_ref[...]
     ones = jnp.ones((8, width), jnp.float32)
     col_norms = [outer_rows(ones, p * p)[:1] for p in points]
@@ -191,97 +191,85 @@
     def schur(rows, rows_norm, rows_known, panel):
         inner = outer_rows(rows, points[panel])
         kernel = jnp.exp((rows_norm + col_norms[panel] - 2.0 * inner) * scale)
-        return kernel - outer_rows(rows_known, knowns[panel])
-
-    top = schur(points[0], norms[0], knowns[0], 0) + ridge
+        return kernel - product(rows_known, knowns[panel])
+
+    first_known, second_known = knowns[0].T, knowns[1].T
+    top = schur(points[0], norms[0], first_known, 0) + ridge
     first = factor_inverse(top)
     inverse_ref[0] = first
-    side = schur(points[1], norms[1], knowns[1], 0)
-    low = schur(points[1], norms[1], knowns[1], 1) + ridge
+    side = schur(points[1], norms[1], second_known, 0)
+    low = schur(points[1], norms[1], second_known, 1) + ridge
     below = outer_rows(side, first)
     inverse_ref[1] = factor_inverse(low - outer_rows(below, below))
+    known = known_ref[2].T
     first_rows = schur(embeddings, row_norms, known, 0)
-    first_rows = first_rows + jnp.where(flags_ref[1] == 0, ridge, 0.0)
+    first_rows = first_rows + jnp.where(my_block == 0, ridge, 0.0)
     second_rows = schur(embeddings, row_norms, known, 1)
-    second_rows = second_rows + jnp.where(flags_ref[1] == 1, ridge, 0.0)
+    second_rows = second_rows + jnp.where(my_block == 1, ridge, 0.0)
     first_panel = outer_rows(first_rows, first)
     second_rows = second_rows - outer_rows(first_panel, below)
-    columns = first_ref.shape[1]
-    own = pl.ds(pl.multiple_of(flags_ref[2] * columns, 8), columns)
-    first_ref[...] = outer_rows(first_rows, inverse_ref[0, own, :])
-    second = outer_rows(second_rows, inverse_ref[1, own, :])
-    second_ref[...] = jnp.where(flags_ref[1] < 1, 0.0, second)
-
-
-def finish(flags, mine, other, embeddings, parts):
+    own = pl.ds(pl.multiple_of(role * columns, 8), columns)
+    out_ref[0] = outer_rows(inverse_ref[0, own, :], first_rows)
+    second = outer_rows(inverse_ref[1, own, :], second_rows)
+    out_ref[1] = jnp.where(my_block < 1, 0.0, second)
+
+
+def finish(block_of, mine, other, embeddings, parts):
     size, width = embeddings.shape
-    known = parts.shape[1]
-    columns = size // lax.axis_size("role")
-    out = jax.ShapeDtypeStruct((size, columns), jnp.float32)
+    columns, known = parts[0].shape
     whole = pl.BlockSpec(memory_space=pltpu.VMEM)
     return pl.pallas_call(
         finish_kernel,
-        in_specs=[pl.BlockSpec(memory_space=pltpu.SMEM)] + [whole] * 4,
-        out_specs=(whole, whole),
-        out_shape=(out, out),
+        in_specs=[pl.BlockSpec(memory_space=pltpu.SMEM)] + [whole] * 7,
+        out_specs=whole,
+        out_shape=jax.ShapeDtypeStruct((2, columns, size), jnp.float32),
         scratch_shapes=[
             pltpu.VMEM((2, size, width), jnp.float32),
-            pltpu.VMEM((2, size, known), jnp.float32),
+            pltpu.VMEM((3, size, size), jnp.float32),
             pltpu.VMEM((2, size, size), jnp.float32),
         ],
+        compiler_params=pltpu.CompilerParams(vmem_limit_bytes=24 * 2**20),
         name="finish",
-    )(flags, mine, other, embeddings, parts)
-
-
-def broadcast_panels(payload, known_wide, owners):
+    )(block_of, mine, other, embeddings, *parts)
+
+
+def broadcast_panels(payload, known, block_of):
     far_count, near_count = lax.axis_size("far"), lax.axis_size("near")
     x_count, core_count = lax.axis_size("x"), lax.axis_size("core")
+    role_count = lax.axis_size("role")
     rows, width = payload.shape
     groups = near_count * x_count
     high, half = rows // groups, width // core_count
+    blocks = block_of.reshape(x_count, far_count, near_count, core_count)
+    blocks = lax.dynamic_index_in_dim(blocks, lax.axis_index("far"), 1, keepdims=False)
+    blocks = blocks.transpose(1, 0, 2).reshape(-1, 1, 1)
     pieces = payload.reshape(groups, high, core_count, half)
     pieces = pieces.transpose(0, 2, 1, 3).reshape(groups * core_count, high, half)
     seen = exchange(pieces, ("near", "x", "core"))
-    parts = copies_from(known_wide, "role")
-    seen, parts = lax.optimization_barrier((seen, parts))
-    sources, fars = [], []
-    for owner in owners:
-        core, place = owner % core_count, owner // core_count
-        near, place = place % near_count, place // near_count
-        far, x = place % far_count, place // far_count
-        sources.append((near * x_count + x) * core_count + core)
-        fars.append(far)
-    own = jnp.concatenate([pick(seen, source) for source in sources], axis=0)
+    own = jnp.concatenate(
+        [jnp.sum(jnp.where(blocks == panel, seen, 0.0), axis=0) for panel in range(2)], axis=0
+    )
+    own, known = lax.optimization_barrier((own, known))
+    parts = [known] + [
+        lax.ppermute(known, "role", [(i, (i + step) % role_count) for i in range(role_count)])
+        for step in range(1, role_count)
+    ]
     seen = copies_from(own, ("far", "near"))
-    seen = seen.reshape(far_count, near_count, len(owners) * high, half)
-    strips = [pick(seen, far) for far in fars]
-    sub = lax.broadcasted_iota(jnp.int32, strips[0].shape, 1)
-    strip = jnp.where(sub < high, strips[0], strips[1])
+    strip = jnp.sum(seen.reshape(far_count, near_count, *own.shape), axis=0)
+    strip, *parts = lax.optimization_barrier((strip, *parts))
     mine = copies_from(strip, ("role", "x"))
     other = lax.ppermute(mine, "core", [(0, 1), (1, 0)])
     return mine, other, parts
 
 
 def on_device(embeddings, earlier_factor, block_of):
-    size = embeddings.shape[0]
-    role_count = lax.axis_size("role")
-    columns = size // role_count
+    columns = embeddings.shape[0] // lax.axis_size("role")
     role = lax.axis_index("role")
-    slot = lax.axis_index(ROWS)
-    my_block = lax.dynamic_index_in_dim(block_of, slot, 0, keepdims=False)
-    slots = jnp.arange(block_of.shape[0], dtype=jnp.int32)
-    owners = [jnp.sum(jnp.where(block_of == panel, slots, 0)) for panel in range(2)]
-
     own_points = lax.dynamic_slice_in_dim(embeddings, role * columns, columns, 0)
-    known_wide = jnp.concatenate(
-        [earlier_factor[g * columns : (g + 1) * columns] for g in range(role_count)], axis=1
-    )
-    payload = jnp.concatenate([own_points, known_wide], axis=1)
-    mine, other, parts = broadcast_panels(payload, known_wide, owners)
-    flags = jnp.stack([lax.axis_index("core"), my_block, role])
-    parts = parts.reshape(size, -1)
-    first_panel, second_panel = finish(flags, mine, other, embeddings, parts)
-    return jnp.stack([first_panel, second_panel], axis=1)
+    known = earlier_factor.T
+    payload = jnp.concatenate([own_points, known], axis=1)
+    mine, other, parts = broadcast_panels(payload, known, block_of)
+    return finish(block_of, mine, other, embeddings, parts).transpose(2, 0, 1)
 
 
 def solution(mesh):

time: 132 us -> 120 us (0.909)
  waiting for transfers between devices: 25.8 us -> 20.4 us
  between operations: 5.28 us -> 0.18 us
  local copies, waits for them, and re-layouts: 7.45 us -> 3.54 us
  starting transfers between devices: 34.2 us -> 38 us
  blocking collectives: 22.7 us -> 24.9 us
  other arithmetic: 3.12 us -> 1.12 us
    ppermute x0 -> x3, starting transfers between devices: none -> 9.5 us  [broadcast_panels(): lax.ppermute(known, 'role', [(i, (i + step) % role_count) for i in range(...]
    all_to_all x3 -> x2, waiting for transfers between devices: 25.2 us -> 17.8 us  [exchange(): return lax.all_to_all(array, axis, 0, 0, tiled=True)]
    all_to_all x3 -> x2, starting transfers between devices: 27.8 us -> 22.1 us  [exchange(): return lax.all_to_all(array, axis, 0, 0, tiled=True)]
    another operation x2 -> x0, other arithmetic: 2.34 us -> none  [the longest x1 1.36 us: on_device(): flags = jnp.stack([lax.axis_index('core'), my_block, role])]
    all_to_all x1, blocking collectives: 22.7 us -> 24.9 us  [exchange(): return lax.all_to_all(array, axis, 0, 0, tiled=True)]
    ppermute x1, waiting for transfers between devices: 0.61 us -> 2.64 us  [broadcast_panels(): other = lax.ppermute(mine, 'core', [(0, 1), (1, 0)])]
  transfers between devices with their start and end apart: 4 -> 6, of which waited for: 4 -> 3; matrix products, arithmetic and copies ran while one was open for 4% -> 1% of each run, Pallas kernels for 0% -> 0%
where the time goes in v2:
time: 120 us
  starting transfers between devices  38 us (32%)
  Pallas kernels  31.6 us (26%)
  blocking collectives  24.9 us (21%)
  waiting for transfers between devices  20.4 us (17%)
  local copies, waits for them, and re-layouts  3.54 us (3%)
    pallas_call x1, Pallas kernels, finish(): pl.pallas_call(finish_kernel, in_specs=[pl.BlockSpec(memory_space=pltpu.S...  31.6 us
    all_to_all x1, blocking collectives, exchange(): return lax.all_to_all(array, axis, 0, 0, tiled=True)  24.9 us
    all_to_all x2, starting transfers between devices, exchange(): return lax.all_to_all(array, axis, 0, 0, tiled=True)  22.1 us
    all_to_all x2, waiting for transfers between devices, exchange(): return lax.all_to_all(array, axis, 0, 0, tiled=True)  17.8 us
    ppermute x3, starting transfers between devices, broadcast_panels(): lax.ppermute(known, 'role', [(i, (i + step) % role_count) for i in range(...  9.5 us
    ppermute x1, starting transfers between devices, broadcast_panels(): other = lax.ppermute(mine, 'core', [(0, 1), (1, 0)])  6.36 us
    ppermute x1, waiting for transfers between devices, broadcast_panels(): other = lax.ppermute(mine, 'core', [(0, 1), (1, 0)])  2.64 us
  transfers between devices with their start and end apart: 6, of which 3 were waited for; matrix products, arithmetic and copies ran while one was open for 1% of the time, Pallas kernels for 0%

profile of v2, /device:TPU:1, one launch (start us, length us, event | category | flops | bytes accessed | tf_op | source)
XLA Modules:
  0.0 119.7 jit_solution(471557100636339973)
XLA Ops:
  0.0 1.0 constant_dynamic-slice_fusion
  1.0 0.9 pad_maximum_fusion
  1.9 0.2 reshape.38
  2.0 0.8 copy.20
  2.8 10.4 %all-to-all-start = ((f32[32,4,640]{2,1,0:T(4,128)}), f32[32,4,640]{2,1,0:T(4,128)S(1)}, u32[]{:S(2)}, u32[]{:S(2)}) async-start(f32[32,4,640]{2,1,0:T(4,128)} %bitcast.4), calls=%async_computation | async-start | bytes 655360 | tf_op jit(solution)/shard_map/all_to_all | solution.py:38
  13.2 0.2 reshape.37
  13.4 0.1 copy.22
  13.5 0.1 copy.21
  13.7 0.1 eq.49
  13.8 0.1 copy.19
  13.9 0.1 eq.44
  14.0 11.8 %all-to-all-done = f32[32,4,640]{2,1,0:T(4,128)S(1)} async-done(((f32[32,4,640]{2,1,0:T(4,128)}), f32[32,4,640]{2,1,0:T(4,128)S(1)}, u32[]{:S(2)}, u32[]{:S(2)}) %all-to-all-start) | async-done | bytes 327712 | tf_op jit(solution)/shard_map/all_to_all | solution.py:38
  25.7 0.2 select_reduce_fusion.1
  26.0 0.7 broadcast_in_dim.33
  26.7 11.7 %all-to-all-start.1 = ((f32[16,8,640]{2,1,0:T(8,128)}), f32[16,8,640]{2,1,0:T(8,128)S(1)}, u32[]{:S(2)}, u32[]{:S(2)}) async-start(f32[16,8,640]{2,1,0:T(8,128)} %broadcast_in_dim.33), calls=%async_computation.1 | async-start | bytes 655360 | tf_op jit(solution)/shard_map/all_to_all | solution.py:38
  38.5 4.6 %collective-permute-start.2 = (f32[64,256]{1,0:T(8,128)S(1)}, f32[64,256]{1,0:T(8,128)S(1)}, u32[]{:S(2)}, u32[]{:S(2)}) collective-permute-start(f32[64,256]{1,0:T(8,128)S(1)} %bitcast.15), channel_id=1, source_target_pairs={{0,384},{128,0},{256,128},{384,256},{1,385},{129,1},{257,129},{385... | collective-permute-start | bytes 196616 | tf_op jit(solution)/shard_map/ppermute | solution.py:254
  43.1 2.3 %collective-permute-start.1 = (f32[64,256]{1,0:T(8,128)S(1)}, f32[64,256]{1,0:T(8,128)S(1)}, u32[]{:S(2)}, u32[]{:S(2)}) collective-permute-start(f32[64,256]{1,0:T(8,128)S(1)} %bitcast.16), channel_id=1, source_target_pairs={{0,256},{128,384},{256,0},{384,128},{1,257},{129,385},{257,1},{385... | collective-permute-start | bytes 196616 | tf_op jit(solution)/shard_map/ppermute | solution.py:254
  45.4 2.6 %collective-permute-start = (f32[64,256]{1,0:T(8,128)S(1)}, f32[64,256]{1,0:T(8,128)S(1)}, u32[]{:S(2)}, u32[]{:S(2)}) collective-permute-start(f32[64,256]{1,0:T(8,128)S(1)} %bitcast.17), channel_id=1, source_target_pairs={{0,128},{128,256},{256,384},{384,0},{1,129},{129,257},{257,385},{3... | collective-permute-start | bytes 196616 | tf_op jit(solution)/shard_map/ppermute | solution.py:254
  48.0 6.0 %all-to-all-done.1 = f32[16,8,640]{2,1,0:T(8,128)S(1)} async-done(((f32[16,8,640]{2,1,0:T(8,128)}), f32[16,8,640]{2,1,0:T(8,128)S(1)}, u32[]{:S(2)}, u32[]{:S(2)}) %all-to-all-start.1) | async-done | bytes 327712 | tf_op jit(solution)/shard_map/all_to_all | solution.py:38
  54.1 0.1 broadcast_in_dim.34
  54.2 24.9 %all_to_all.15.mine_ref = f32[16,4,8,640]{3,2,1,0:T(8,128)S(1)} all-to-all(f32[16,4,8,640]{3,2,1,0:T(8,128)S(1)} %broadcast_in_dim.34), channel_id=1, replica_groups=mesh['role'=4,'x'=4,'far'=4,'near'=4,'core'=2] {'role','x'}, dimensions={0} | all-to-all | bytes 2621440 | tf_op jit(solution)/shard_map/all_to_all | solution.py:38
  79.1 6.4 %collective-permute-start.3 = (f32[16,4,8,640]{3,2,1,0:T(8,128)S(1)}, f32[16,4,8,640]{3,2,1,0:T(8,128)S(1)}, u32[]{:S(2)}, u32[]{:S(2)}) collective-permute-start(f32[16,4,8,640]{3,2,1,0:T(8,128)S(1)} %all_to_all.15.mine_ref), channel_id=1, source_target_pairs={{0,1},{1,0},{2,3},{3,2},{4,5},{5,4},{6,7},{7,6},{8,9},{9,8},{10,11... | collective-permute-start | bytes 3932168 | tf_op jit(solution)/shard_map/ppermute | solution.py:261
  85.5 2.6 %collective-permute-done.3.other_ref = f32[16,4,8,640]{3,2,1,0:T(8,128)S(1)} collective-permute-done((f32[16,4,8,640]{3,2,1,0:T(8,128)S(1)}, f32[16,4,8,640]{3,2,1,0:T(8,128)S(1)}, u32[]{:S(2)}, u32[]{:S(2)}) %collective-permute-start.3) | collective-permute-done | bytes 1310752 | tf_op jit(solution)/shard_map/ppermute | solution.py:261
  88.1 31.6 %finish.1 = f32[2,64,256]{2,1,0:T(8,128)} custom-call(s32[128]{0:T(128)S(1)} %copy-done.2, f32[16,4,8,640]{3,2,1,0:T(8,128)S(1)} %all_to_all.15.mine_ref, f32[16,4,8,640]{3,2,1,0:T(8,128)S(1)} %collective-permute-done.3.other_ref, f32[256,1024]{1,0:T(8,128)S(1)} %copy-done, f32[64,256]{1,0:T(8,128)S(1)} %bitcast.18, ...), custom_call_target="tpu_custom_call" | custom-call | tf_op jit(solution)/shard_map/finish/pallas_call | solution.py:221
  (13 shorter events, 0.1 us)
Async XLA Ops:
  1.0 12.3 %copy-start.2 = (s32[128]{0:T(128)S(1)}, s32[128]{0:T(128)}, u32[]{:S(2)}) copy-start(s32[128]{0:T(128)} %block_ref.1) | copy-start | bytes 1540
  2.0 36.4 %copy-start.1 = (f32[256,64]{0,1:T(8,128)S(1)}, f32[256,64]{0,1:T(8,128)}, u32[]{:S(2)}) copy-start(f32[256,64]{0,1:T(8,128)} %param.4) | copy-start | bytes 196612
  2.8 22.9 %all-to-all-start = ((f32[32,4,640]{2,1,0:T(4,128)}), f32[32,4,640]{2,1,0:T(4,128)S(1)}, u32[]{:S(2)}, u32[]{:S(2)}) async-start(f32[32,4,640]{2,1,0:T(4,128)} %bitcast.4), calls=%async_computation | async-start | bytes 655360 | tf_op jit(solution)/shard_map/all_to_all | solution.py:38
  26.7 27.3 %all-to-all-start.1 = ((f32[16,8,640]{2,1,0:T(8,128)}), f32[16,8,640]{2,1,0:T(8,128)S(1)}, u32[]{:S(2)}, u32[]{:S(2)}) async-start(f32[16,8,640]{2,1,0:T(8,128)} %broadcast_in_dim.33), calls=%async_computation.1 | async-start | bytes 655360 | tf_op jit(solution)/shard_map/all_to_all | solution.py:38
  38.5 15.6 %collective-permute-start.2 = (f32[64,256]{1,0:T(8,128)S(1)}, f32[64,256]{1,0:T(8,128)S(1)}, u32[]{:S(2)}, u32[]{:S(2)}) collective-permute-start(f32[64,256]{1,0:T(8,128)S(1)} %bitcast.15), channel_id=1, source_target_pairs={{0,384},{128,0},{256,128},{384,256},{1,385},{129,1},{257,129},{385... | collective-permute-start | bytes 196616 | tf_op jit(solution)/shard_map/ppermute | solution.py:254
  43.1 10.9 %collective-permute-start.1 = (f32[64,256]{1,0:T(8,128)S(1)}, f32[64,256]{1,0:T(8,128)S(1)}, u32[]{:S(2)}, u32[]{:S(2)}) collective-permute-start(f32[64,256]{1,0:T(8,128)S(1)} %bitcast.16), channel_id=1, source_target_pairs={{0,256},{128,384},{256,0},{384,128},{1,257},{129,385},{257,1},{385... | collective-permute-start | bytes 196616 | tf_op jit(solution)/shard_map/ppermute | solution.py:254
  45.4 8.7 %collective-permute-start = (f32[64,256]{1,0:T(8,128)S(1)}, f32[64,256]{1,0:T(8,128)S(1)}, u32[]{:S(2)}, u32[]{:S(2)}) collective-permute-start(f32[64,256]{1,0:T(8,128)S(1)} %bitcast.17), channel_id=1, source_target_pairs={{0,128},{128,256},{256,384},{384,0},{1,129},{129,257},{257,385},{3... | collective-permute-start | bytes 196616 | tf_op jit(solution)/shard_map/ppermute | solution.py:254
  54.2 33.9 %copy-start = (f32[256,1024]{1,0:T(8,128)S(1)}, f32[256,1024]{1,0:T(8,128)}, u32[]{:S(2)}) copy-start(f32[256,1024]{1,0:T(8,128)} %embeddings_ref.1) | copy-start | bytes 3145732
  79.1 9.0 %collective-permute-start.3 = (f32[16,4,8,640]{3,2,1,0:T(8,128)S(1)}, f32[16,4,8,640]{3,2,1,0:T(8,128)S(1)}, u32[]{:S(2)}, u32[]{:S(2)}) collective-permute-start(f32[16,4,8,640]{3,2,1,0:T(8,128)S(1)} %all_to_all.15.mine_ref), channel_id=1, source_target_pairs={{0,1},{1,0},{2,3},{3,2},{4,5},{5,4},{6,7},{7,6},{8,9},{9,8},{10,11... | collective-permute-start | bytes 3932168 | tf_op jit(solution)/shard_map/ppermute | solution.py:261

commit v3 on v2

--- a/solution.py
+++ b/solution.py
@@ -10,8 +10,10 @@
 
 highest = lax.Precision.HIGHEST
 ridge_weight = 1.0
-TILE = 64
+TILE = 128
 STEP = 8
+CHUNK = 256
+EVERY = 3
 
 
 def outer_rows(rows, columns):
@@ -47,29 +49,32 @@
     return lax.dynamic_index_in_dim(array, index, 0, keepdims=False)
 
 
-def small_inverse(block):
+def small_inverse(block, beside):
     size = block.shape[0]
-    row_ids = lax.broadcasted_iota(jnp.int32, (size, size), 0)
-    col_ids = lax.broadcasted_iota(jnp.int32, (size, size), 1)
-    identity = (row_ids == col_ids).astype(jnp.float32)
-    both = jnp.concatenate([block, identity], axis=1)
-    tiles = [both[STEP * g : STEP * g + STEP] for g in range(size // STEP)]
+    tiles = [block[STEP * g : STEP * g + STEP] for g in range(size // STEP)]
     shape = tiles[0].shape
-    lane = lax.broadcasted_iota(jnp.int32, shape, 0)
-    pivots = [None] * len(tiles)
+    sub = lax.broadcasted_iota(jnp.int32, shape, 0)
+    lane = lax.broadcasted_iota(jnp.int32, shape, 1)
+    done = []
     for g in range(len(tiles)):
-        later = range(g, len(tiles))
         start = STEP * g
+        later = range(g + 1, len(tiles))
+        here = (lane >= start) & (lane < start + STEP)
         cols = [
-            {h: jnp.broadcast_to(tiles[h][:, start + q : start + q + 1], shape) for h in later}
+            {
+                h: jnp.broadcast_to(tiles[h][:, start + q : start + q + 1], shape)
+                for h in range(g, len(tiles))
+            }
             for q in range(STEP)
         ]
-        rows = [jnp.broadcast_to(tiles[g][a : a + 1], shape) for a in range(STEP)]
+        own = jnp.where(here, (lane == start + sub).astype(jnp.float32), tiles[g])
+        rows = [jnp.broadcast_to(own[a : a + 1], shape) for a in range(STEP)]
         piv = [
             [jnp.broadcast_to(cols[b][g][a : a + 1], shape) for b in range(a + 1)]
             for a in range(STEP)
         ]
         inverse = [None] * STEP
+        ratio = [[None] * STEP for _ in range(STEP)]
         for q in range(STEP):
             if q % 2 == 0:
                 inverse[q] = 1.0 / piv[q][q]
@@ -77,30 +82,33 @@
                     piv[q][q] * piv[q + 1][q + 1] - piv[q + 1][q] * piv[q + 1][q]
                 )
             for a in range(q + 1, STEP):
-                ratio = piv[a][q] * inverse[q]
+                ratio[a][q] = piv[a][q] * inverse[q]
                 for b in range(q + 1, a + 1):
-                    piv[a][b] = piv[a][b] - ratio * piv[b][q]
-                rows[a] = rows[a] - ratio * rows[q]
-                for h in later:
-                    cols[a][h] = cols[a][h] - ratio * cols[q][h]
-        pivots[g] = piv[0][0]
+                    piv[a][b] = piv[a][b] - ratio[a][q] * piv[b][q]
+                rows[a] = rows[a] - ratio[a][q] * rows[q]
+                for h in later[:1]:
+                    cols[a][h] = cols[a][h] - ratio[a][q] * cols[q][h]
+        scale, final = inverse[0], rows[0]
         for q in range(1, STEP):
-            pivots[g] = jnp.where(lane == q, piv[q][q], pivots[g])
+            scale = jnp.where(sub == q, inverse[q], scale)
+            final = jnp.where(sub == q, rows[q], final)
+        done.append(jnp.where(lane < start + STEP, final * jnp.sqrt(scale), 0.0))
+        rows = [rows[q] * inverse[q] for q in range(STEP)]
+        solved = list(rows)
+        for a in range(STEP - 1, 0, -1):
+            for b in range(a):
+                solved[b] = solved[b] - ratio[a][b] * solved[a]
         for h in later:
-            terms = []
-            for q in range(STEP - 1 if h == g else STEP):
-                factor = cols[q][h] * inverse[q]
-                if h == g:
-                    factor = jnp.where(lane > q, factor, 0.0)
-                terms.append(factor * rows[q])
+            use = rows if h == g + 1 else solved
+            terms = [cols[q][h] * use[q] for q in range(STEP)]
             while len(terms) > 1:
-                terms = [sum(terms[i : i + 2]) for i in range(0, len(terms), 2)]
-            tiles[h] = tiles[h] - terms[0]
-    done = [t[:, size:] * lax.rsqrt(p[:, size:]) for t, p in zip(tiles, pivots)]
+                terms = [terms[i] + terms[i + 1] for i in range(0, len(terms), 2)]
+            tiles[h] = jnp.where(here, 0.0, tiles[h]) - terms[0]
+        beside()
     return jnp.concatenate(done, axis=0)
 
 
-def factor_inverse(whole):
+def factor_inverse(whole, beside):
     count = whole.shape[0] // TILE
     left = [
         [whole[TILE * i : TILE * i + TILE, TILE * j : TILE * j + TILE] for j in range(count)]
@@ -109,7 +117,7 @@
     lower = [[None] * count for _ in range(count)]
     inverse = [[jnp.zeros((TILE, TILE), jnp.float32)] * count for _ in range(count)]
     for k in range(count):
-        inverse[k][k] = small_inverse(left[k][k])
+        inverse[k][k] = small_inverse(left[k][k], beside)
         for i in range(k + 1, count):
             lower[i][k] = outer_rows(left[i][k], inverse[k][k])
         for i in range(k + 1, count):
@@ -143,6 +151,8 @@
     points_ref,
     known_ref,
     inverse_ref,
+    turned_ref,
+    rows_ref,
 ):
     size, width = embeddings_ref.shape
     half = mine_ref.shape[-1]
@@ -180,37 +190,76 @@
     row_ids = lax.broadcasted_iota(jnp.int32, (size, size), 0)
     col_ids = lax.broadcasted_iota(jnp.int32, (size, size), 1)
     ridge = jnp.where(row_ids == col_ids, ridge_weight, 0.0)
-    points = [points_ref[p] for p in range(2)]
-    knowns = [known_ref[p] for p in range(2)]
-    embeddings = embeddings_ref[...]
     ones = jnp.ones((8, width), jnp.float32)
-    col_norms = [outer_rows(ones, p * p)[:1] for p in points]
-    norms = [jnp.sum(p * p, axis=1, keepdims=True) for p in points]
-    row_norms = jnp.sum(embeddings * embeddings, axis=1, keepdims=True)
-
-    def schur(rows, rows_norm, rows_known, panel):
-        inner = outer_rows(rows, points[panel])
-        kernel = jnp.exp((rows_norm + col_norms[panel] - 2.0 * inner) * scale)
-        return kernel - product(rows_known, knowns[panel])
-
-    first_known, second_known = knowns[0].T, knowns[1].T
-    top = schur(points[0], norms[0], first_known, 0) + ridge
-    first = factor_inverse(top)
+    col_norms = [outer_rows(ones, points_ref[p] * points_ref[p])[:1] for p in range(2)]
+    turned_ref[0] = known_ref[0].T
+
+    def schur(row_ref, panel, turned, start, count):
+        chunk = pl.ds(start, count)
+        rows = row_ref[chunk, :]
+        norms = jnp.sum(rows * rows, axis=1, keepdims=True)
+        inner = outer_rows(rows, points_ref[panel])
+        kernel = jnp.exp((norms + col_norms[panel] - 2.0 * inner) * scale)
+        return kernel - product(turned_ref[turned, chunk, :], known_ref[panel])
+
+    def schur_piece(target, row_ref, panel, turned, start):
+        def emit():
+            rows_ref[target, pl.ds(start, CHUNK), :] = schur(row_ref, panel, turned, start, CHUNK)
+
+        return emit
+
+    def turn(index):
+        def emit():
+            turned_ref[index] = known_ref[index].T
+
+        return emit
+
+    def spread(work):
+        count, state = len(work), [0, 0]
+
+        def beside():
+            state[0] += 1
+            if state[0] % EVERY == 0 and state[1] < count:
+                work[state[1]]()
+                state[1] += 1
+
+        def rest():
+            while state[1] < count:
+                work[state[1]]()
+                state[1] += 1
+
+        return beside, rest
+
+    starts = range(0, size, CHUNK)
+    jobs = [(0, points_ref.at[1], 0, 1), (1, points_ref.at[1], 1, 1)]
+    jobs += [(2, embeddings_ref, 0, 2), (3, embeddings_ref, 1, 2)]
+    work = [turn(1), turn(2)]
+    work += [schur_piece(*job, start) for job in jobs for start in starts]
+    beside, rest = spread(work)
+    first = factor_inverse(schur(points_ref.at[0], 0, 0, 0, size) + ridge, beside)
+    rest()
     inverse_ref[0] = first
-    side = schur(points[1], norms[1], second_known, 0)
-    low = schur(points[1], norms[1], second_known, 1) + ridge
-    below = outer_rows(side, first)
-    inverse_ref[1] = factor_inverse(low - outer_rows(below, below))
-    known = known_ref[2].T
-    first_rows = schur(embeddings, row_norms, known, 0)
-    first_rows = first_rows + jnp.where(my_block == 0, ridge, 0.0)
-    second_rows = schur(embeddings, row_norms, known, 1)
-    second_rows = second_rows + jnp.where(my_block == 1, ridge, 0.0)
-    first_panel = outer_rows(first_rows, first)
-    second_rows = second_rows - outer_rows(first_panel, below)
+    below = outer_rows(rows_ref[0], first)
     own = pl.ds(pl.multiple_of(role * columns, 8), columns)
-    out_ref[0] = outer_rows(inverse_ref[0, own, :], first_rows)
-    second = outer_rows(inverse_ref[1, own, :], second_rows)
+    first_rows = rows_ref[2] + jnp.where(my_block == 0, ridge, 0.0)
+
+    def panel_piece(start):
+        def emit():
+            chunk = slice(start, start + CHUNK)
+            panel = outer_rows(first_rows[chunk], first)
+            second_rows = rows_ref[3, pl.ds(start, CHUNK), :] - outer_rows(panel, below)
+            here = jnp.where(my_block == 1, ridge[chunk], 0.0)
+            rows_ref[3, pl.ds(start, CHUNK), :] = second_rows + here
+
+        return emit
+
+    def first_output():
+        out_ref[0] = outer_rows(inverse_ref[0, own, :], first_rows)
+
+    beside, rest = spread([panel_piece(start) for start in starts] + [first_output])
+    inverse_ref[1] = factor_inverse(rows_ref[1] + ridge - outer_rows(below, below), beside)
+    rest()
+    second = outer_rows(inverse_ref[1, own, :], rows_ref[3])
     out_ref[1] = jnp.where(my_block < 1, 0.0, second)
 
 
@@ -227,6 +276,8 @@
             pltpu.VMEM((2, size, width), jnp.float32),
             pltpu.VMEM((3, size, size), jnp.float32),
             pltpu.VMEM((2, size, size), jnp.float32),
+            pltpu.VMEM((3, size, size), jnp.float32),
+            pltpu.VMEM((4, size, size), jnp.float32),
         ],
         compiler_params=pltpu.CompilerParams(vmem_limit_bytes=24 * 2**20),
         name="finish",
@@ -249,14 +300,13 @@
     own = jnp.concatenate(
         [jnp.sum(jnp.where(blocks == panel, seen, 0.0), axis=0) for panel in range(2)], axis=0
     )
-    own, known = lax.optimization_barrier((own, known))
     parts = [known] + [
         lax.ppermute(known, "role", [(i, (i + step) % role_count) for i in range(role_count)])
         for step in range(1, role_count)
     ]
+    own, *parts = lax.optimization_barrier((own, *parts))
     seen = copies_from(own, ("far", "near"))
     strip = jnp.sum(seen.reshape(far_count, near_count, *own.shape), axis=0)
-    strip, *parts = lax.optimization_barrier((strip, *parts))
     mine = copies_from(strip, ("role", "x"))
     other = lax.ppermute(mine, "core", [(0, 1), (1, 0)])
     return mine, other, parts

time: 120 us -> 112 us (0.933)
  the two profiles are of different devices: /device:TPU:1 before, /device:TPU:33 now
where the time goes in v3:
time: 112 us
  blocking collectives  54.8 us (49%)
  Pallas kernels  23.8 us (21%)
  starting transfers between devices  23.6 us (21%)
  waiting for transfers between devices  5.24 us (5%)
  local copies, waits for them, and re-layouts  2.83 us (3%)
  other arithmetic  1.16 us (1%)
    all_to_all x2, blocking collectives, exchange(): return lax.all_to_all(array, axis, 0, 0, tiled=True)  54.8 us
    pallas_call x1, Pallas kernels, finish(): pl.pallas_call(finish_kernel, in_specs=[pl.BlockSpec(memory_space=pltpu.S...  23.8 us
    all_to_all x1, starting transfers between devices, exchange(): return lax.all_to_all(array, axis, 0, 0, tiled=True)  9.31 us
    ppermute x3, starting transfers between devices, broadcast_panels(): lax.ppermute(known, 'role', [(i, (i + step) % role_count) for i in range(...  9.09 us
    ppermute x1, starting transfers between devices, broadcast_panels(): other = lax.ppermute(mine, 'core', [(0, 1), (1, 0)])  5.17 us
    ppermute x1, waiting for transfers between devices, broadcast_panels(): other = lax.ppermute(mine, 'core', [(0, 1), (1, 0)])  2.64 us
  transfers between devices with their start and end apart: 5, of which 3 were waited for; matrix products, arithmetic and copies ran while one was open for 1% of the time, Pallas kernels for 0%

profile of v3, /device:TPU:33, one launch (start us, length us, event | category | flops | bytes accessed | tf_op | source)
XLA Modules:
  0.0 111.7 jit_solution(17015976811989423059)
XLA Ops:
  0.0 1.0 constant_dynamic-slice_fusion
  1.0 0.9 pad_maximum_fusion
  1.9 0.2 reshape.38
  2.1 0.8 copy.20
  2.9 9.3 %all-to-all-start = ((f32[32,4,640]{2,1,0:T(4,128)}), f32[32,4,640]{2,1,0:T(4,128)S(1)}, u32[]{:S(2)}, u32[]{:S(2)}) async-start(f32[32,4,640]{2,1,0:T(4,128)} %bitcast.4), calls=%async_computation | async-start | bytes 655360 | tf_op jit(solution)/shard_map/all_to_all | solution.py:40
  12.2 4.2 %collective-permute-start.2 = (f32[64,256]{1,0:T(8,128)S(1)}, f32[64,256]{1,0:T(8,128)S(1)}, u32[]{:S(2)}, u32[]{:S(2)}) collective-permute-start(f32[64,256]{1,0:T(8,128)S(1)} %bitcast.15), channel_id=1, source_target_pairs={{0,384},{128,0},{256,128},{384,256},{1,385},{129,1},{257,129},{385... | collective-permute-start | bytes 196616 | tf_op jit(solution)/shard_map/ppermute | solution.py:304
  16.5 2.3 %collective-permute-start.1 = (f32[64,256]{1,0:T(8,128)S(1)}, f32[64,256]{1,0:T(8,128)S(1)}, u32[]{:S(2)}, u32[]{:S(2)}) collective-permute-start(f32[64,256]{1,0:T(8,128)S(1)} %bitcast.16), channel_id=1, source_target_pairs={{0,256},{128,384},{256,0},{384,128},{1,257},{129,385},{257,1},{385... | collective-permute-start | bytes 196616 | tf_op jit(solution)/shard_map/ppermute | solution.py:304
  18.7 2.6 %collective-permute-start = (f32[64,256]{1,0:T(8,128)S(1)}, f32[64,256]{1,0:T(8,128)S(1)}, u32[]{:S(2)}, u32[]{:S(2)}) collective-permute-start(f32[64,256]{1,0:T(8,128)S(1)} %bitcast.17), channel_id=1, source_target_pairs={{0,128},{128,256},{256,384},{384,0},{1,129},{129,257},{257,385},{3... | collective-permute-start | bytes 196616 | tf_op jit(solution)/shard_map/ppermute | solution.py:304
  21.4 0.2 reshape.37
  21.5 0.1 copy.22
  21.7 0.1 copy.21
  21.8 0.1 eq.49
  21.9 0.1 copy.19
  22.0 0.1 eq.44
  22.1 1.7 %all-to-all-done = f32[32,4,640]{2,1,0:T(4,128)S(1)} async-done(((f32[32,4,640]{2,1,0:T(4,128)}), f32[32,4,640]{2,1,0:T(4,128)S(1)}, u32[]{:S(2)}, u32[]{:S(2)}) %all-to-all-start) | async-done | bytes 327712 | tf_op jit(solution)/shard_map/all_to_all | solution.py:40
  23.8 0.2 select_reduce_fusion.1
  24.1 0.9 collective-permute-done.near_ref
  25.0 31.8 %all_to_all.15 = f32[16,8,640]{2,1,0:T(8,128)S(1)} all-to-all(f32[16,8,640]{2,1,0:T(8,128)S(1)} %broadcast_in_dim.33), channel_id=1, replica_groups=mesh['role'=4,'x'=4,'far'=4,'near'=4,'core'=2] {'far','near'}, dimensions={0} | all-to-all | bytes 655360 | tf_op jit(solution)/shard_map/all_to_all | solution.py:40
  56.8 0.1 broadcast_in_dim.34
  56.9 0.0 copy-start
  56.9 23.1 %all_to_all.16.mine_ref = f32[16,4,8,640]{3,2,1,0:T(8,128)S(1)} all-to-all(f32[16,4,8,640]{3,2,1,0:T(8,128)S(1)} %broadcast_in_dim.34), channel_id=1, replica_groups=mesh['role'=4,'x'=4,'far'=4,'near'=4,'core'=2] {'role','x'}, dimensions={0} | all-to-all | bytes 2621440 | tf_op jit(solution)/shard_map/all_to_all | solution.py:40
  80.0 5.2 %collective-permute-start.3 = (f32[16,4,8,640]{3,2,1,0:T(8,128)S(1)}, f32[16,4,8,640]{3,2,1,0:T(8,128)S(1)}, u32[]{:S(2)}, u32[]{:S(2)}) collective-permute-start(f32[16,4,8,640]{3,2,1,0:T(8,128)S(1)} %all_to_all.16.mine_ref), channel_id=1, source_target_pairs={{0,1},{1,0},{2,3},{3,2},{4,5},{5,4},{6,7},{7,6},{8,9},{9,8},{10,11... | collective-permute-start | bytes 3932168 | tf_op jit(solution)/shard_map/ppermute | solution.py:311
  85.2 2.6 %collective-permute-done.3.other_ref = f32[16,4,8,640]{3,2,1,0:T(8,128)S(1)} collective-permute-done((f32[16,4,8,640]{3,2,1,0:T(8,128)S(1)}, f32[16,4,8,640]{3,2,1,0:T(8,128)S(1)}, u32[]{:S(2)}, u32[]{:S(2)}) %collective-permute-start.3) | collective-permute-done | bytes 1310752 | tf_op jit(solution)/shard_map/ppermute | solution.py:311
  87.8 23.8 %finish.1 = f32[2,64,256]{2,1,0:T(8,128)} custom-call(s32[128]{0:T(128)S(1)} %copy-done.2, f32[16,4,8,640]{3,2,1,0:T(8,128)S(1)} %all_to_all.16.mine_ref, f32[16,4,8,640]{3,2,1,0:T(8,128)S(1)} %collective-permute-done.3.other_ref, f32[256,1024]{1,0:T(8,128)S(1)} %copy-done, f32[64,256]{1,0:T(8,128)S(1)} %bitcast.18, ...), custom_call_target="tpu_custom_call" | custom-call | tf_op jit(solution)/shard_map/finish/pallas_call | solution.py:270
  (12 shorter events, 0.1 us)
Async XLA Ops:
  1.0 11.3 %copy-start.1 = (f32[256,64]{0,1:T(8,128)S(1)}, f32[256,64]{0,1:T(8,128)}, u32[]{:S(2)}) copy-start(f32[256,64]{0,1:T(8,128)} %param.4) | copy-start | bytes 196612
  1.0 20.4 %copy-start.2 = (s32[128]{0:T(128)S(1)}, s32[128]{0:T(128)}, u32[]{:S(2)}) copy-start(s32[128]{0:T(128)} %block_ref.1) | copy-start | bytes 1540
  2.9 20.9 %all-to-all-start = ((f32[32,4,640]{2,1,0:T(4,128)}), f32[32,4,640]{2,1,0:T(4,128)S(1)}, u32[]{:S(2)}, u32[]{:S(2)}) async-start(f32[32,4,640]{2,1,0:T(4,128)} %bitcast.4), calls=%async_computation | async-start | bytes 655360 | tf_op jit(solution)/shard_map/all_to_all | solution.py:40
  12.2 11.8 %collective-permute-start.2 = (f32[64,256]{1,0:T(8,128)S(1)}, f32[64,256]{1,0:T(8,128)S(1)}, u32[]{:S(2)}, u32[]{:S(2)}) collective-permute-start(f32[64,256]{1,0:T(8,128)S(1)} %bitcast.15), channel_id=1, source_target_pairs={{0,384},{128,0},{256,128},{384,256},{1,385},{129,1},{257,129},{385... | collective-permute-start | bytes 196616 | tf_op jit(solution)/shard_map/ppermute | solution.py:304
  16.5 7.6 %collective-permute-start.1 = (f32[64,256]{1,0:T(8,128)S(1)}, f32[64,256]{1,0:T(8,128)S(1)}, u32[]{:S(2)}, u32[]{:S(2)}) collective-permute-start(f32[64,256]{1,0:T(8,128)S(1)} %bitcast.16), channel_id=1, source_target_pairs={{0,256},{128,384},{256,0},{384,128},{1,257},{129,385},{257,1},{385... | collective-permute-start | bytes 196616 | tf_op jit(solution)/shard_map/ppermute | solution.py:304
  18.7 6.2 %collective-permute-start = (f32[64,256]{1,0:T(8,128)S(1)}, f32[64,256]{1,0:T(8,128)S(1)}, u32[]{:S(2)}, u32[]{:S(2)}) collective-permute-start(f32[64,256]{1,0:T(8,128)S(1)} %bitcast.17), channel_id=1, source_target_pairs={{0,128},{128,256},{256,384},{384,0},{1,129},{129,257},{257,385},{3... | collective-permute-start | bytes 196616 | tf_op jit(solution)/shard_map/ppermute | solution.py:304
  56.9 30.9 %copy-start = (f32[256,1024]{1,0:T(8,128)S(1)}, f32[256,1024]{1,0:T(8,128)}, u32[]{:S(2)}) copy-start(f32[256,1024]{1,0:T(8,128)} %embeddings_ref.1) | copy-start | bytes 3145732
  80.0 7.8 %collective-permute-start.3 = (f32[16,4,8,640]{3,2,1,0:T(8,128)S(1)}, f32[16,4,8,640]{3,2,1,0:T(8,128)S(1)}, u32[]{:S(2)}, u32[]{:S(2)}) collective-permute-start(f32[16,4,8,640]{3,2,1,0:T(8,128)S(1)} %all_to_all.16.mine_ref), channel_id=1, source_target_pairs={{0,1},{1,0},{2,3},{3,2},{4,5},{5,4},{6,7},{7,6},{8,9},{9,8},{10,11... | collective-permute-start | bytes 3932168 | tf_op jit(solution)/shard_map/ppermute | solution.py:311

commit v4 on v3

--- a/solution.py
+++ b/solution.py
@@ -292,6 +292,8 @@
     groups = near_count * x_count
     high, half = rows // groups, width // core_count
     blocks = block_of.reshape(x_count, far_count, near_count, core_count)
+    holds = [jnp.any(blocks == panel, axis=(0, 2, 3)) for panel in range(2)]
+    apart = jnp.logical_not(jnp.any(holds[0] & holds[1]))
     blocks = lax.dynamic_index_in_dim(blocks, lax.axis_index("far"), 1, keepdims=False)
     blocks = blocks.transpose(1, 0, 2).reshape(-1, 1, 1)
     pieces = payload.reshape(groups, high, core_count, half)
@@ -305,8 +307,22 @@
         for step in range(1, role_count)
     ]
     own, *parts = lax.optimization_barrier((own, *parts))
-    seen = copies_from(own, ("far", "near"))
-    strip = jnp.sum(seen.reshape(far_count, near_count, *own.shape), axis=0)
+
+    def gathered(strip):
+        seen = copies_from(strip, ("far", "near"))
+        return seen.reshape(far_count, near_count, *strip.shape)
+
+    def whole_strips(own):
+        return jnp.sum(gathered(own), axis=0)
+
+    def half_strips(own):
+        seen = gathered(own[:high] + own[high:])
+        chosen = [
+            jnp.sum(jnp.where(held.reshape(-1, 1, 1, 1), seen, 0.0), axis=0) for held in holds
+        ]
+        return jnp.concatenate(chosen, axis=1)
+
+    strip = lax.cond(apart, half_strips, whole_strips, own)
     mine = copies_from(strip, ("role", "x"))
     other = lax.ppermute(mine, "core", [(0, 1), (1, 0)])
     return mine, other, parts

time: 112 us -> 106 us (0.946)
  the two profiles are of different devices: /device:TPU:33 before, /device:TPU:1 now
where the time goes in v4:
time: 106 us; the launch traced here: 105 us
  blocking collectives  44.4 us (42%)
  starting transfers between devices  27.5 us (26%)
  Pallas kernels  23.8 us (22%)
  waiting for transfers between devices  3.69 us (3%)
  local copies, waits for them, and re-layouts  2.82 us (3%)
  other arithmetic  2.2 us (2%)
    all_to_all x2, blocking collectives, exchange(): return lax.all_to_all(array, axis, 0, 0, tiled=True)  44.4 us
    pallas_call x1, Pallas kernels, finish(): pl.pallas_call(finish_kernel, in_specs=[pl.BlockSpec(memory_space=pltpu.S...  23.8 us
    all_to_all x1, starting transfers between devices, exchange(): return lax.all_to_all(array, axis, 0, 0, tiled=True)  10.4 us
    ppermute x3, starting transfers between devices, broadcast_panels(): lax.ppermute(known, 'role', [(i, (i + step) % role_count) for i in range(...  9.14 us
    ppermute x1, starting transfers between devices, broadcast_panels(): other = lax.ppermute(mine, 'core', [(0, 1), (1, 0)])  8 us
    ppermute x1, waiting for transfers between devices, broadcast_panels(): other = lax.ppermute(mine, 'core', [(0, 1), (1, 0)])  2.64 us
  transfers between devices with their start and end apart: 5, of which 2 were waited for; matrix products, arithmetic and copies ran while one was open for 2% of the time, Pallas kernels for 0%

profile of v4, /device:TPU:1, one launch (start us, length us, event | category | flops | bytes accessed | tf_op | source)
XLA Modules:
  0.0 105.4 jit_solution(8538808709686058929)
XLA Ops:
  0.0 1.0 constant_dynamic-slice_fusion
  1.0 0.9 pad_maximum_fusion.1
  1.9 0.2 reshape.46
  2.1 0.8 copy.20
  2.9 10.4 %all-to-all-start.2 = ((f32[32,4,640]{2,1,0:T(4,128)}), f32[32,4,640]{2,1,0:T(4,128)S(1)}, u32[]{:S(2)}, u32[]{:S(2)}) async-start(f32[32,4,640]{2,1,0:T(4,128)} %bitcast.6), calls=%async_computation.2 | async-start | bytes 655360 | tf_op jit(solution)/shard_map/all_to_all | solution.py:40
  13.3 4.3 %collective-permute-start.2 = (f32[64,256]{1,0:T(8,128)S(1)}, f32[64,256]{1,0:T(8,128)S(1)}, u32[]{:S(2)}, u32[]{:S(2)}) collective-permute-start(f32[64,256]{1,0:T(8,128)S(1)} %bitcast.16), channel_id=1, source_target_pairs={{0,384},{128,0},{256,128},{384,256},{1,385},{129,1},{257,129},{385... | collective-permute-start | bytes 196616 | tf_op jit(solution)/shard_map/ppermute | solution.py:306
  17.6 2.3 %collective-permute-start.1 = (f32[64,256]{1,0:T(8,128)S(1)}, f32[64,256]{1,0:T(8,128)S(1)}, u32[]{:S(2)}, u32[]{:S(2)}) collective-permute-start(f32[64,256]{1,0:T(8,128)S(1)} %bitcast.17), channel_id=1, source_target_pairs={{0,256},{128,384},{256,0},{384,128},{1,257},{129,385},{257,1},{385... | collective-permute-start | bytes 196616 | tf_op jit(solution)/shard_map/ppermute | solution.py:306
  19.8 2.6 %collective-permute-start = (f32[64,256]{1,0:T(8,128)S(1)}, f32[64,256]{1,0:T(8,128)S(1)}, u32[]{:S(2)}, u32[]{:S(2)}) collective-permute-start(f32[64,256]{1,0:T(8,128)S(1)} %bitcast.18), channel_id=1, source_target_pairs={{0,128},{128,256},{256,384},{384,0},{1,129},{129,257},{257,385},{3... | collective-permute-start | bytes 196616 | tf_op jit(solution)/shard_map/ppermute | solution.py:306
  22.5 0.2 reshape.45
  22.6 0.1 copy.22
  22.7 0.2 compare_reduce_fusion
  23.0 0.6 and_reduce_fusion
  24.3 0.1 copy.21
  24.5 0.1 copy.19
  24.8 1.0 all-to-all-done.2
  25.8 0.2 select_reduce_fusion.3
  26.1 24.6 %conditional.1 = (f32[4,8,640]{2,1,0:T(8,128)S(1)}) conditional(s32[]{:T(128)} %convert_element_type.3, f32[8,640]{1,0:T(8,128)S(1)} %pad_maximum_fusion.2, (pred[4]{0:T(512)(128)(4,1)S(1)}, f32[8,640]{1,0:T(8,128)S(1)}, pred[4]{0:T(512)(128)(4,1)S(1)}) %tuple.13), branch_computations={%region_5.7_spmd, %region_7.10_spmd} | conditional | flops 166400 | bytes 1413132 | solution.py:325
  26.1 24.3 %all_to_all.19 = f32[16,4,640]{2,1,0:T(4,128)S(1)} all-to-all(f32[16,4,640]{2,1,0:T(4,128)S(1)} %broadcast_in_dim.47), channel_id=1, replica_groups=mesh['role'=4,'x'=4,'far'=4,'near'=4,'core'=2] {'far','near'}, dimensions={0} | all-to-all | bytes 327680 | tf_op jit(solution)/shard_map/cond/branch_1_fun/all_to_all | solution.py:40
  50.4 0.1 select_reduce_fusion.1
  50.6 0.1 broadcast_in_dim.57
  50.8 20.1 %all_to_all.20.mine_ref = f32[16,4,8,640]{3,2,1,0:T(8,128)S(1)} all-to-all(f32[16,4,8,640]{3,2,1,0:T(8,128)S(1)} %broadcast_in_dim.57), channel_id=1, replica_groups=mesh['role'=4,'x'=4,'far'=4,'near'=4,'core'=2] {'role','x'}, dimensions={0} | all-to-all | bytes 2621440 | tf_op jit(solution)/shard_map/all_to_all | solution.py:40
  70.9 8.0 %collective-permute-start.3 = (f32[16,4,8,640]{3,2,1,0:T(8,128)S(1)}, f32[16,4,8,640]{3,2,1,0:T(8,128)S(1)}, u32[]{:S(2)}, u32[]{:S(2)}) collective-permute-start(f32[16,4,8,640]{3,2,1,0:T(8,128)S(1)} %all_to_all.20.mine_ref), channel_id=1, source_target_pairs={{0,1},{1,0},{2,3},{3,2},{4,5},{5,4},{6,7},{7,6},{8,9},{9,8},{10,11... | collective-permute-start | bytes 3932168 | tf_op jit(solution)/shard_map/ppermute | solution.py:327
  78.9 2.6 %collective-permute-done.3.other_ref = f32[16,4,8,640]{3,2,1,0:T(8,128)S(1)} collective-permute-done((f32[16,4,8,640]{3,2,1,0:T(8,128)S(1)}, f32[16,4,8,640]{3,2,1,0:T(8,128)S(1)}, u32[]{:S(2)}, u32[]{:S(2)}) %collective-permute-start.3) | collective-permute-done | bytes 1310752 | tf_op jit(solution)/shard_map/ppermute | solution.py:327
  81.5 23.8 %finish.1 = f32[2,64,256]{2,1,0:T(8,128)} custom-call(s32[128]{0:T(128)S(1)} %copy-done.2, f32[16,4,8,640]{3,2,1,0:T(8,128)S(1)} %all_to_all.20.mine_ref, f32[16,4,8,640]{3,2,1,0:T(8,128)S(1)} %collective-permute-done.3.other_ref, f32[256,1024]{1,0:T(8,128)S(1)} %copy-done, f32[64,256]{1,0:T(8,128)S(1)} %bitcast.19, ...), custom_call_target="tpu_custom_call" | custom-call | tf_op jit(solution)/shard_map/finish/pallas_call | solution.py:270
  (17 shorter events, 0.3 us)
Async XLA Ops:
  1.0 12.3 %copy-start.1 = (f32[256,64]{0,1:T(8,128)S(1)}, f32[256,64]{0,1:T(8,128)}, u32[]{:S(2)}) copy-start(f32[256,64]{0,1:T(8,128)} %param.6) | copy-start | bytes 196612
  1.0 21.5 %copy-start.2 = (s32[128]{0:T(128)S(1)}, s32[128]{0:T(128)}, u32[]{:S(2)}) copy-start(s32[128]{0:T(128)} %block_ref.1) | copy-start | bytes 1540
  2.9 22.9 %all-to-all-start.2 = ((f32[32,4,640]{2,1,0:T(4,128)}), f32[32,4,640]{2,1,0:T(4,128)S(1)}, u32[]{:S(2)}, u32[]{:S(2)}) async-start(f32[32,4,640]{2,1,0:T(4,128)} %bitcast.6), calls=%async_computation.2 | async-start | bytes 655360 | tf_op jit(solution)/shard_map/all_to_all | solution.py:40
  13.3 12.8 %collective-permute-start.2 = (f32[64,256]{1,0:T(8,128)S(1)}, f32[64,256]{1,0:T(8,128)S(1)}, u32[]{:S(2)}, u32[]{:S(2)}) collective-permute-start(f32[64,256]{1,0:T(8,128)S(1)} %bitcast.16), channel_id=1, source_target_pairs={{0,384},{128,0},{256,128},{384,256},{1,385},{129,1},{257,129},{385... | collective-permute-start | bytes 196616 | tf_op jit(solution)/shard_map/ppermute | solution.py:306
  17.6 8.5 %collective-permute-start.1 = (f32[64,256]{1,0:T(8,128)S(1)}, f32[64,256]{1,0:T(8,128)S(1)}, u32[]{:S(2)}, u32[]{:S(2)}) collective-permute-start(f32[64,256]{1,0:T(8,128)S(1)} %bitcast.17), channel_id=1, source_target_pairs={{0,256},{128,384},{256,0},{384,128},{1,257},{129,385},{257,1},{385... | collective-permute-start | bytes 196616 | tf_op jit(solution)/shard_map/ppermute | solution.py:306
  19.8 6.2 %collective-permute-start = (f32[64,256]{1,0:T(8,128)S(1)}, f32[64,256]{1,0:T(8,128)S(1)}, u32[]{:S(2)}, u32[]{:S(2)}) collective-permute-start(f32[64,256]{1,0:T(8,128)S(1)} %bitcast.18), channel_id=1, source_target_pairs={{0,128},{128,256},{256,384},{384,0},{1,129},{129,257},{257,385},{3... | collective-permute-start | bytes 196616 | tf_op jit(solution)/shard_map/ppermute | solution.py:306
  50.7 30.8 %copy-start = (f32[256,1024]{1,0:T(8,128)S(1)}, f32[256,1024]{1,0:T(8,128)}, u32[]{:S(2)}) copy-start(f32[256,1024]{1,0:T(8,128)} %embeddings_ref.1) | copy-start | bytes 3145732
  70.9 10.7 %collective-permute-start.3 = (f32[16,4,8,640]{3,2,1,0:T(8,128)S(1)}, f32[16,4,8,640]{3,2,1,0:T(8,128)S(1)}, u32[]{:S(2)}, u32[]{:S(2)}) collective-permute-start(f32[16,4,8,640]{3,2,1,0:T(8,128)S(1)} %all_to_all.20.mine_ref), channel_id=1, source_target_pairs={{0,1},{1,0},{2,3},{3,2},{4,5},{5,4},{6,7},{7,6},{8,9},{9,8},{10,11... | collective-permute-start | bytes 3932168 | tf_op jit(solution)/shard_map/ppermute | solution.py:327
